TPU v7x, 128 devices: a whole 4x4x4 slice. The times are simulated.
128 devices in a mesh: blk: 64 (over z, x, y), mc: 2 (over core).
Axes of the slice: x: 4, y: 4, z: 4, core: 2. Of those that a mesh axis runs over, the one named last changes fastest.
Arguments:
- batch_ids: int32 [2048], P('blk'), may hold values from 0 to 16383, as said below
- cond_ids: int32 [2048, 3], P('blk'), may hold values from 0 to 16383, as said below
- home: int32 [16384], replicated, may hold values from 0 to 16383, as said below
- latent: bfloat16 [16384, 32, 256], P('blk', 'mc'), may hold values from -6 to 6
- diag_factor: bfloat16 [2048, 256, 256], P('blk'), may hold values from -0.375 to 0.375
- cond_factor: bfloat16 [2048, 3, 256, 256], P('blk'), may hold values from -0.375 to 0.375
- obs: float32 [2048, 256], P('blk'), may hold values from -6 to 6
- noise_prec: float32 [], replicated, may hold values from 0.5 to 2
Outputs:
- mean_grad: float32 [16384, 256], P('blk', 'mc')
Inputs may be any that keep to these rules, and one draw needn't show every extreme that they name: home is a permutation; block b is stored at position home[b], on index home[b] // 256 of blk. `batch_ids`: of the 128 blocks named by one index's rows (each row's own block and its conditioning blocks, repeats counted), at most 5 are stored on any one index of blk. `cond_ids`: counted together with batch_ids as stated there.
All inputs are finite; a program needn't handle non-finite values.
Results may differ from a plain program's by a relative error of at most 0.0029.
Values may be sent and summed in bfloat16 or wider, within the bound.
No kernel may reach another device: no remote copies, remote signals or barrier semaphores. Data moves between devices by JAX's collectives and lax.ppermute only.
A program may use at most 64 MiB of HBM per device.

v0:
```python
import jax
import jax.numpy as jnp
from jax import lax
from jax.sharding import PartitionSpec as P

freedom = 4.0


def body(batch_ids, cond_ids, home, latent, diag_factor, cond_factor, obs, noise_prec):
    owners = lax.axis_size("blk")
    per_owner = latent.shape[0]
    draw_count = latent.shape[1]
    block_width = latent.shape[2]
    row_count = batch_ids.shape[0]
    want_count = 4 * row_count
    capacity = max(2, 10 * row_count // owners)
    inverse_draws = 1.0 / (draw_count * lax.axis_size("mc"))
    block_ids = jnp.concatenate([batch_ids[:, None], cond_ids], axis=1).reshape(-1)
    wanted = home[block_ids]
    dest_dev = wanted // per_owner
    slot_idx = wanted % per_owner
    earlier = jnp.arange(want_count)[:, None] > jnp.arange(want_count)[None, :]
    same_dest = dest_dev[:, None] == dest_dev[None, :]
    rank_idx = jnp.sum(same_dest & earlier, axis=1)
    send_spot = dest_dev * capacity + rank_idx
    outbox = (
        jnp.full((owners * capacity,), -1, jnp.int32)
        .at[send_spot]
        .set(slot_idx)
        .reshape(owners, capacity)
    )
    in_slots = lax.all_to_all(outbox, "blk", split_axis=0, concat_axis=0, tiled=True)
    is_valid = in_slots >= 0
    outgoing = latent[jnp.maximum(in_slots, 0)]
    fetched = lax.all_to_all(outgoing, "blk", split_axis=0, concat_axis=0, tiled=True)
    picked = fetched.reshape(owners * capacity, draw_count, block_width)[send_spot]
    picked = picked.reshape(row_count, 4, draw_count, block_width)
    own_panel = picked[:, 0]
    near_panel = picked[:, 1:]
    lower_mask = jnp.arange(block_width)[:, None] >= jnp.arange(block_width)[None, :]
    lower_diag = jnp.where(lower_mask[None, :, :], diag_factor, jnp.zeros_like(diag_factor))
    whitened = jnp.einsum("rsj,rij->rsi", own_panel, lower_diag, preferred_element_type=jnp.float32)
    whitened = whitened + jnp.einsum(
        "rksj,rkij->rsi", near_panel, cond_factor, preferred_element_type=jnp.float32
    )
    scored = (freedom + 1.0) * whitened / (freedom + whitened * whitened)
    white_low = scored.astype(jnp.bfloat16)
    back_diag = jnp.einsum("rsi,rij->rj", white_low, lower_diag, preferred_element_type=jnp.float32)
    likely = noise_prec * jnp.sum(obs[:, None, :] - own_panel.astype(jnp.float32), axis=1)
    self_term = (likely - back_diag) * inverse_draws
    cond_term = (
        -jnp.einsum("rsi,rkij->rkj", white_low, cond_factor, preferred_element_type=jnp.float32)
        * inverse_draws
    )
    grad_terms = jnp.concatenate([self_term[:, None, :], cond_term], axis=1).reshape(
        want_count, block_width
    )
    target_slot = jnp.where(is_valid, in_slots, per_owner).reshape(-1)
    outbox_terms = (
        jnp.zeros((owners * capacity, block_width), jnp.float32).at[send_spot].set(grad_terms)
    )
    inbox_terms = lax.all_to_all(
        outbox_terms.reshape(owners, capacity, block_width),
        "blk",
        split_axis=0,
        concat_axis=0,
        tiled=True,
    )
    stored = (
        jnp.zeros((per_owner, block_width), jnp.float32)
        .at[target_slot]
        .add(inbox_terms.reshape(-1, block_width), mode="drop")
    )
    return lax.psum_scatter(stored, "mc", scatter_dimension=1, tiled=True)


def solution(mesh):
    placed = (
        P("blk"),
        P("blk", None),
        P(),
        P("blk", "mc", None),
        P("blk", None, None),
        P("blk", None, None, None),
        P("blk", None),
        P(),
    )
    return jax.shard_map(
        body, mesh=mesh, in_specs=placed, out_specs=P("blk", "mc"), check_vma=False
    )
```

profile of v0, /device:TPU:0, one launch (start us, length us, event | category | flops | bytes accessed | tf_op | source)
XLA Modules:
  0.0 131.5 jit_solution(15543225446557591097)
XLA Ops:
  6.5 0.0 copy-start
  6.5 0.8 pad_add_fusion
  7.4 0.1 copy.16
  7.5 0.1 reshape.192
  7.6 1.8 %gather_fusion = s32[128]{0:T(128)S(1)} fusion(s32[16384]{0:T(1024)} %param.10, s32[1024]{0:T(1024)S(1)} %pad_clamp_fusion.2), kind=kCustom, calls=%fused_computation | custom fusion | bytes 1536 | tf_op jit(solution)/shard_map/gather | solution.py:19
  9.4 0.2 convert_reduce_fusion.1
  9.6 1.0 scatter_custom_fusion
  10.6 0.1 all_to_all.14
  10.7 20.8 %all_to_all.22 = s32[64,1,5]{2,1,0:T(1,128)S(1)} all-to-all(s32[64,1,5]{2,1,0:T(1,128)S(1)} %bitcast.60), channel_id=1, replica_groups=mesh['blk'=64,'mc'=2] {'blk'}, dimensions={0} | all-to-all | bytes 2560 | tf_op jit(solution)/shard_map/all_to_all | solution.py:32
  31.6 0.5 broadcast.231
  32.1 0.8 maximum_reduce_fusion
  32.9 0.1 reshape.208
  33.0 0.0 copy-done
  33.1 3.0 %gather_fusion.1 = bf16[320,16,256]{2,1,0:T(8,128)(2,1)} fusion(bf16[256,16,256]{2,1,0:T(8,128)(2,1)S(1)} %copy-done, s32[1024]{0:T(1024)S(1)} %pad_clamp_fusion.1), kind=kCustom, calls=%fused_computation.1 | custom fusion | bytes 5244160 | tf_op jit(solution)/shard_map/gather | solution.py:34
  36.1 5.6 %all-to-all-start.1 = ((bf16[64,5,16,256]{3,2,1,0:T(8,128)(2,1)}), bf16[64,5,16,256]{3,2,1,0:T(8,128)(2,1)}, u32[]{:S(2)}, u32[]{:S(2)}) async-start(bf16[64,5,16,256]{3,2,1,0:T(8,128)(2,1)} %bitcast.54), calls=%async_computation.1 | async-start | bytes 5242880 | tf_op jit(solution)/shard_map/all_to_all | solution.py:35
  42.4 33.2 %all-to-all-done.1 = bf16[64,5,16,256]{3,2,1,0:T(8,128)(2,1)} async-done(((bf16[64,5,16,256]{3,2,1,0:T(8,128)(2,1)}), bf16[64,5,16,256]{3,2,1,0:T(8,128)(2,1)}, u32[]{:S(2)}, u32[]{:S(2)}) %all-to-all-start.1) | async-done | bytes 2621472 | tf_op jit(solution)/shard_map/all_to_all | solution.py:35
  75.6 2.4 %gather_fusion.2 = bf16[128,16,256]{2,1,0:T(8,128)(2,1)S(1)} fusion(bf16[320,16,256]{2,1,0:T(8,128)(2,1)} %bitcast.7, s32[1024]{0:T(1024)S(1)} %pad_clamp_fusion), kind=kCustom, calls=%fused_computation.2 | custom fusion | bytes 2097664 | tf_op jit(solution)/shard_map/gather | solution.py:36
  78.0 0.0 slice-start
  78.0 4.3 %fusion.1 = f32[32,16,256]{2,1,0:T(8,128)} fusion(bf16[32,256,256]{2,1,0:T(8,128)(2,1)} %param.12, pred[256,256]{1,0:T(8,128)(4,1)S(1)} %iota_compare_fusion, bf16[32,4,16,256]{3,2,1,0:T(8,128)(2,1)S(1)} %bitcast.55), kind=kOutput, calls=%fused_computation.8 | convolution fusion | flops 69206016 | bytes 5046272 | tf_op jit(solution)/shard_map/rsj,rij->rsi/dot_general | solution.py:42
  82.3 0.0 slice-start.1
  82.4 0.0 slice-start.2
  82.4 8.2 %convert_reduce_fusion = bf16[32,256]{1,0:T(8,128)(2,1)S(1)} fusion(f32[32,16,256]{2,1,0:T(8,128)} %fusion.1, bf16[32,4,16,256]{3,2,1,0:T(8,128)(2,1)S(1)} %bitcast.56, bf16[32,3,256,256]{3,2,1,0:T(8,128)(2,1)} %param.13), kind=kOutput, calls=%fused_computation.13 | convolution fusion | flops 202366976 | bytes 14172160 | tf_op jit(solution)/shard_map/rksj,rkij->rsi/dot_general | solution.py:43
  90.5 0.0 copy-start.1
  90.5 2.9 %fusion = f32[32,1,256]{2,1,0:T(1,128)S(1)} fusion(bf16[32,256,256]{2,1,0:T(8,128)(2,1)} %param.12, pred[256,256]{1,0:T(8,128)(4,1)S(1)} %iota_compare_fusion, bf16[32,256,1]{1,0,2:T(8,128)(2,1)S(1)} %bitcast.58), kind=kOutput, calls=%fused_computation.7 | convolution fusion | flops 6291456 | bytes 4308992 | tf_op jit(solution)/shard_map/rsi,rij->rj/dot_general | solution.py:48
  93.4 0.0 copy-done.1
  93.4 0.1 subtract_reduce_fusion
  93.6 0.0 slice-done
  93.6 0.0 slice-done.1
  93.6 0.0 slice-done.2
  93.6 1.7 %fusion.12 = f32[32,1,3,256]{3,1,2,0:T(1,128)S(1)} fusion(bf16[32,3,256,256]{3,2,1,0:T(8,128)(2,1)S(1)} %bitcast.53, bf16[32,256,1,1]{1,0,2,3:T(8,128)(2,1)S(1)} %bitcast.59), kind=kOutput, calls=%fused_computation.30 | convolution fusion | flops 12582912 | bytes 12697600 | tf_op jit(solution)/shard_map/rsi,rkij->rkj/dot_general | solution.py:52
  95.4 0.1 pad_maximum_fusion
  95.5 1.1 scatter_custom_fusion.1
  96.6 0.8 reshape.196
  97.5 6.2 %all-to-all-start.2 = ((f32[64,5,256]{2,1,0:T(8,128)}), f32[64,5,256]{2,1,0:T(8,128)S(1)}, u32[]{:S(2)}, u32[]{:S(2)}) async-start(f32[64,5,256]{2,1,0:T(8,128)} %reshape.196), calls=%async_computation.2 | async-start | bytes 1048576 | tf_op jit(solution)/shard_map/all_to_all | solution.py:62
  103.6 0.0 reduce-scatter.2.cloned.1.call-start
  103.7 0.1 all_to_all.16
  103.9 11.7 %all-to-all-done.2 = f32[64,5,256]{2,1,0:T(8,128)S(1)} async-done(((f32[64,5,256]{2,1,0:T(8,128)}), f32[64,5,256]{2,1,0:T(8,128)S(1)}, u32[]{:S(2)}, u32[]{:S(2)}) %all-to-all-start.2) | async-done | bytes 327712 | tf_op jit(solution)/shard_map/all_to_all | solution.py:62
  115.5 0.1 reshape.242
  115.6 2.9 %scatter_custom_fusion.2 = f32[256,256]{1,0:T(8,128)} fusion(s32[320]{0:T(512)S(1)} %fusion.15, f32[320,256]{1,0:T(8,128)S(1)} %reshape.242, f32[]{:T(128)} %constant.17.clone.1), kind=kCustom, calls=%fused_computation.23 | custom fusion | flops 81920 | bytes 262148 | tf_op jit(solution)/shard_map/scatter-add | solution.py:72
  118.5 0.0 reduce-scatter.2.cloned.1.call-update
  118.6 6.1 %reduce-scatter.2.cloned.1.call-done = f32[256,128]{1,0:T(8,128)} async-done(((f32[256,256]{1,0:T(8,128)}), f32[256,128]{1,0:T(8,128)}) %reduce-scatter.2.cloned.1.call-update) | async-done | bytes 131088 | tf_op jit(solution)/shard_map/reduce_scatter | solution.py:74
  (13 shorter events, 0.2 us)
Async XLA Ops:
  6.5 26.5 %copy-start = (bf16[256,16,256]{2,1,0:T(8,128)(2,1)S(1)}, bf16[256,16,256]{2,1,0:T(8,128)(2,1)}, u32[]{:S(2)}) copy-start(bf16[256,16,256]{2,1,0:T(8,128)(2,1)} %param.11) | copy-start | bytes 6291460
  36.1 39.5 %all-to-all-start.1 = ((bf16[64,5,16,256]{3,2,1,0:T(8,128)(2,1)}), bf16[64,5,16,256]{3,2,1,0:T(8,128)(2,1)}, u32[]{:S(2)}, u32[]{:S(2)}) async-start(bf16[64,5,16,256]{3,2,1,0:T(8,128)(2,1)} %bitcast.54), calls=%async_computation.1 | async-start | bytes 5242880 | tf_op jit(solution)/shard_map/all_to_all | solution.py:35
  78.0 15.6 %slice-start = ((s8[12582912]{0:T(1024)(128)(4,1)}), s8[4194304]{0:T(1024)(128)(4,1)S(1)}, s32[]{:S(2)}) async-start(s8[12582912]{0:T(1024)(128)(4,1)} %bitcast.52), calls=%async_computation.5 | async-start | bytes 8388608
  82.3 11.3 %slice-start.1 = ((s8[12582912]{0:T(1024)(128)(4,1)}), s8[4194304]{0:T(1024)(128)(4,1)S(1)}, s32[]{:S(2)}) async-start(s8[12582912]{0:T(1024)(128)(4,1)} %bitcast.52), calls=%async_computation.6 | async-start | bytes 8388608
  82.4 11.3 %slice-start.2 = ((s8[12582912]{0:T(1024)(128)(4,1)}), s8[4194304]{0:T(1024)(128)(4,1)S(1)}, s32[]{:S(2)}) async-start(s8[12582912]{0:T(1024)(128)(4,1)} %bitcast.52), calls=%async_computation.7 | async-start | bytes 8388608
  90.5 2.9 %copy-start.1 = (f32[32,256]{1,0:T(8,128)S(1)}, f32[32,256]{1,0:T(8,128)}, u32[]{:S(2)}) copy-start(f32[32,256]{1,0:T(8,128)} %param.14) | copy-start | bytes 98308
  97.5 18.1 %all-to-all-start.2 = ((f32[64,5,256]{2,1,0:T(8,128)}), f32[64,5,256]{2,1,0:T(8,128)S(1)}, u32[]{:S(2)}, u32[]{:S(2)}) async-start(f32[64,5,256]{2,1,0:T(8,128)} %reshape.196), calls=%async_computation.2 | async-start | bytes 1048576 | tf_op jit(solution)/shard_map/all_to_all | solution.py:62
  103.6 21.0 %reduce-scatter.2.cloned.1.call-start = ((), (), s32[]{:S(2)}) async-start(), calls=%async_computation.4 | async-start | bytes 393216 | tf_op jit(solution)/shard_map/reduce_scatter | solution.py:74
Sparse Core Ops, SparseCore 0:
  118.7 5.9 reduce-scatter.1
where the time goes:
time: 133 us; the launch traced here: 132 us
  waiting for transfers between devices  51.1 us (38%)
  blocking collectives  20.8 us (16%)
  matrix products  17.1 us (13%)
  between operations  14.3 us (11%)
  starting transfers between devices  11.8 us (9%)
  local copies, waits for them, and re-layouts  11.4 us (9%)
  other arithmetic  5.12 us (4%)
    all_to_all x1, waiting for transfers between devices, body(): lax.all_to_all(outgoing, 'blk', split_axis=0, concat_axis=0, tiled=True)  33.2 us
    all_to_all x1, blocking collectives, body(): lax.all_to_all(outbox, 'blk', split_axis=0, concat_axis=0, tiled=True)  20.8 us
    all_to_all x1, waiting for transfers between devices, body(): lax.all_to_all(outbox_terms.reshape(owners, capacity, block_width), 'blk'...  11.7 us
    dot_general x1, matrix products, body(): jnp.einsum('rksj,rkij->rsi', near_panel, cond_factor, preferred_element_t...  8.18 us
    all_to_all x1, starting transfers between devices, body(): lax.all_to_all(outbox_terms.reshape(owners, capacity, block_width), 'blk'...  6.17 us
    reduce_scatter x1, waiting for transfers between devices, body(): return lax.psum_scatter(stored, 'mc', scatter_dimension=1, tiled=True)  6.13 us
    all_to_all x1, starting transfers between devices, body(): lax.all_to_all(outgoing, 'blk', split_axis=0, concat_axis=0, tiled=True)  5.56 us
    dot_general x1, matrix products, body(): jnp.einsum('rsj,rij->rsi', own_panel, lower_diag, preferred_element_type=...  4.34 us
  transfers between devices with their start and end apart: 3, of which 3 were waited for; matrix products, arithmetic and copies ran while one was open for 0% of the time, Pallas kernels for 0%

commit v1 on v0

v1 whole, which is shorter than its diff:
```python
import functools

import jax
import jax.numpy as jnp
from jax import lax
from jax.experimental import pallas as pl
from jax.experimental.pallas import tpu as pltpu
from jax.sharding import PartitionSpec as P

freedom = 4.0
vmem = pl.BlockSpec(memory_space=pltpu.VMEM)
smem = pl.BlockSpec(memory_space=pltpu.SMEM)
budget = pltpu.CompilerParams(vmem_limit_bytes=48 * 1024 * 1024)
iota = lax.broadcasted_iota


def plan_kernel(owners, capacity, per_owner, own_ref, near_ref, home_ref, outbox_ref, spot_ref):
    home = home_ref[...]
    high_count, low_count = home.shape
    dest_table = (home // per_owner).astype(jnp.float32).T.astype(jnp.bfloat16)
    slot_table = (home % per_owner).astype(jnp.float32).T.astype(jnp.bfloat16)
    rows = own_ref.shape[1]
    earlier = (iota(jnp.int32, (rows, rows), 0) < iota(jnp.int32, (rows, rows), 1)).astype(jnp.bfloat16)
    high_iota = iota(jnp.int32, (high_count, rows), 0)
    low_iota = iota(jnp.int32, (low_count, rows), 0)
    dest_iota = iota(jnp.int32, (owners, rows), 0)
    before = jnp.zeros((owners, 1), jnp.float32)
    marks = [jnp.zeros((owners, 1), jnp.float32) for _ in range(capacity)]
    for which in range(1 + near_ref.shape[0]):
        ids = own_ref[...] if which == 0 else near_ref[which - 1 : which, :]
        high_hot = (high_iota == ids // low_count).astype(jnp.bfloat16)
        low_hot = low_iota == ids % low_count
        dest = jnp.dot(dest_table, high_hot, preferred_element_type=jnp.float32)
        dest = jnp.sum(jnp.where(low_hot, dest, 0.0), axis=0, keepdims=True)
        slot = jnp.dot(slot_table, high_hot, preferred_element_type=jnp.float32)
        slot = jnp.sum(jnp.where(low_hot, slot, 0.0), axis=0, keepdims=True)
        asked = dest_iota == dest.astype(jnp.int32)
        ranks = before + jnp.dot(asked.astype(jnp.bfloat16), earlier, preferred_element_type=jnp.float32)
        before = before + jnp.sum(asked.astype(jnp.float32), axis=1, keepdims=True)
        for k in range(capacity):
            taken = asked & (ranks == float(k))
            marks[k] = marks[k] + jnp.sum(jnp.where(taken, slot + 1.0, 0.0), axis=1, keepdims=True)
        rank = jnp.sum(jnp.where(asked, ranks, 0.0), axis=0, keepdims=True)
        spot_ref[which : which + 1, :] = (dest * 8.0 + rank).astype(jnp.int32)
    lanes = iota(jnp.int32, (owners, outbox_ref.shape[2]), 1)
    outbox = jnp.full(lanes.shape, -1.0, jnp.float32)
    for k in range(capacity):
        outbox = jnp.where(lanes == k, marks[k] - 1.0, outbox)
    outbox_ref[:, 0, :] = outbox.astype(jnp.int32)


def pack_kernel(slots_ref, latent_ref, out_ref):
    owners, capacity = out_ref.shape[:2]

    def step(dev, carry):
        for k in range(capacity):
            out_ref[dev, k] = latent_ref[jnp.maximum(slots_ref[dev, 0, k], 0)]
        return carry

    lax.fori_loop(0, owners, step, 0, unroll=4)


def score_kernel(spot_ref, fetched_ref, diag_ref, cond_ref, sums_ref):
    row_count, width = diag_ref.shape[:2]
    lower = iota(jnp.int32, (width, width), 0) >= iota(jnp.int32, (width, width), 1)
    turned = (((1,), (1,)), ((), ()))

    def step(row, carry):
        spots = [spot_ref[which, row] for which in range(1 + cond_ref.shape[1])]
        panels = [fetched_ref[spot // 8, spot % 8] for spot in spots]
        factor = jnp.where(lower, diag_ref[row], jnp.zeros((), diag_ref.dtype))
        whitened = lax.dot_general(panels[0], factor, turned, preferred_element_type=jnp.float32)
        for which in range(cond_ref.shape[1]):
            whitened = whitened + lax.dot_general(
                panels[which + 1], cond_ref[row, which], turned, preferred_element_type=jnp.float32
            )
        scored = (freedom + 1.0) * whitened / (freedom + whitened * whitened)
        scored = scored.astype(jnp.bfloat16).astype(jnp.float32)
        sums_ref[0, pl.ds(row, 1), :] = jnp.sum(scored, axis=0, keepdims=True)
        sums_ref[1, pl.ds(row, 1), :] = jnp.sum(panels[0].astype(jnp.float32), axis=0, keepdims=True)
        return carry

    lax.fori_loop(0, row_count, step, 0, unroll=2)


def term_kernel(draws, spot_ref, noise_ref, mine_ref, other_ref, obs_ref, diag_ref, cond_ref, out_ref, likely_ref):
    row_count, width = diag_ref.shape[:2]
    half = out_ref.shape[2]
    first = pl.multiple_of(lax.axis_index("mc") * half, half)
    lower = iota(jnp.int32, (width, half), 0) >= iota(jnp.int32, (width, half), 1) + first
    inverse_draws = 1.0 / draws
    which_row = iota(jnp.int32, (16, width), 0)
    out_ref[...] = jnp.zeros_like(out_ref)
    part = pl.ds(first, half)
    owned = mine_ref[1, :, part] + other_ref[1, :, part]
    likely_ref[...] = noise_ref[0, 0] * (obs_ref[:, part] * float(draws) - owned)

    def step(row, carry):
        total = mine_ref[0, pl.ds(row, 1), :] + other_ref[0, pl.ds(row, 1), :]
        coarse = total.astype(jnp.bfloat16).astype(jnp.float32)
        pieces = jnp.where(which_row == 0, coarse, jnp.where(which_row == 1, total - coarse, 0.0))
        pieces = pieces.astype(jnp.bfloat16)
        likely = likely_ref[pl.ds(row, 1), :]
        for which in range(1 + cond_ref.shape[1]):
            if which == 0:
                factor = diag_ref[row, :, part]
                factor = jnp.where(lower, factor, jnp.zeros((), factor.dtype))
            else:
                factor = cond_ref[row, which - 1, :, part]
            back = jnp.dot(pieces, factor, preferred_element_type=jnp.float32)
            back = jnp.sum(back, axis=0, keepdims=True)
            term = (likely - back) * inverse_draws if which == 0 else -back * inverse_draws
            spot = spot_ref[which, row]
            out_ref[spot // 8, pl.ds(spot % 8, 1), :] = term
        return carry

    lax.fori_loop(0, row_count, step, 0, unroll=2)


def gather_kernel(slots_ref, inbox_ref, out_ref):
    owners, capacity, half = inbox_ref.shape
    per_owner = out_ref.shape[0]
    slots = slots_ref[:, 0, :].astype(jnp.float32).T
    places = iota(jnp.int32, (per_owner, owners), 0).astype(jnp.float32)
    total = jnp.zeros((per_owner, half), jnp.float32)
    for k in range(capacity):
        hot = (places == slots[k : k + 1, :]).astype(jnp.bfloat16)
        rest = inbox_ref[:, k, :]
        for _ in range(3):
            piece = rest.astype(jnp.bfloat16)
            rest = rest - piece.astype(jnp.float32)
            total = total + jnp.dot(hot, piece, preferred_element_type=jnp.float32)
    out_ref[...] = total


def body(batch_ids, cond_ids, home, latent, diag_factor, cond_factor, obs, noise_prec):
    owners = lax.axis_size("blk")
    groups = lax.axis_size("mc")
    per_owner, draw_count, width = latent.shape
    row_count = batch_ids.shape[0]
    want_kinds = 1 + cond_ids.shape[1]
    capacity = max(2, 10 * row_count // owners)
    draws = draw_count * groups
    half = width // groups

    def swap(values):
        return lax.all_to_all(values, "blk", split_axis=0, concat_axis=0, tiled=True)

    outbox, spot = pl.pallas_call(
        functools.partial(plan_kernel, owners, capacity, per_owner),
        out_shape=(
            jax.ShapeDtypeStruct((owners, 1, 128), jnp.int32),
            jax.ShapeDtypeStruct((want_kinds, row_count), jnp.int32),
        ),
        in_specs=[vmem] * 3,
        out_specs=(vmem, vmem),
        name="plan",
    )(batch_ids.reshape(1, row_count), cond_ids.T, home.reshape(-1, 128))
    slots = swap(outbox)
    outgoing = pl.pallas_call(
        pack_kernel,
        out_shape=jax.ShapeDtypeStruct((owners, capacity, draw_count, width), latent.dtype),
        in_specs=[smem, vmem],
        out_specs=vmem,
        compiler_params=budget,
        name="pack",
    )(slots, latent)
    fetched = swap(outgoing)
    sums = pl.pallas_call(
        score_kernel,
        out_shape=jax.ShapeDtypeStruct((2, row_count, width), jnp.float32),
        in_specs=[smem, vmem, vmem, vmem],
        out_specs=vmem,
        compiler_params=budget,
        name="score",
    )(spot, fetched, diag_factor, cond_factor)
    others = lax.ppermute(sums, "mc", [(0, 1), (1, 0)])
    terms = pl.pallas_call(
        functools.partial(term_kernel, draws),
        out_shape=jax.ShapeDtypeStruct((owners, capacity, half), jnp.float32),
        in_specs=[smem, smem] + [vmem] * 5,
        out_specs=vmem,
        scratch_shapes=[pltpu.VMEM((row_count, half), jnp.float32)],
        compiler_params=budget,
        name="terms",
    )(spot, noise_prec.reshape(1, 1), sums, others, obs, diag_factor, cond_factor)
    inbox = swap(terms)
    return pl.pallas_call(
        gather_kernel,
        out_shape=jax.ShapeDtypeStruct((per_owner, half), jnp.float32),
        in_specs=[vmem] * 2,
        out_specs=vmem,
        name="collect",
    )(slots, inbox)


def solution(mesh):
    placed = (
        P("blk"),
        P("blk", None),
        P(),
        P("blk", "mc", None),
        P("blk", None, None),
        P("blk", None, None, None),
        P("blk", None),
        P(),
    )
    return jax.shard_map(
        body, mesh=mesh, in_specs=placed, out_specs=P("blk", "mc"), check_vma=False
    )
```

time: 133 us -> 108 us (0.81); the launches traced: 132 us -> 108 us
  blocking collectives: 20.8 us -> 75.8 us
  waiting for transfers between devices: 51.1 us -> 0.59 us
  Pallas kernels: 0 us -> 26.9 us
  matrix products: 17.1 us -> 0 us
  between operations: 14.3 us -> 0.69 us
  starting transfers between devices: 11.8 us -> 0.09 us
  local copies, waits for them, and re-layouts: 11.4 us -> 3.79 us
  other arithmetic: 5.12 us -> 0 us
    all_to_all x1 -> x3, blocking collectives: 20.8 us -> 75.8 us  [swap(): lax.all_to_all(values, 'blk', split_axis=0, concat_axis=0, tiled=True)]
    all_to_all x2 -> x0, waiting for transfers between devices: 44.9 us -> none  [the longest x1 33.2 us: body(): lax.all_to_all(outgoing, 'blk', split_axis=0, concat_axis=0, tiled=True)]
    pallas_call x0 -> x5, Pallas kernels: none -> 26.9 us  [the longest x1 12.5 us: body(): pl.pallas_call(score_kernel, out_shape=jax.ShapeDtypeStruct((2, row_count...]
    dot_general x4 -> x0, matrix products: 17.1 us -> none  [the longest x1 8.18 us: body(): jnp.einsum('rksj,rkij->rsi', near_panel, cond_factor, preferred_element_t...]
    all_to_all x2 -> x0, starting transfers between devices: 11.7 us -> none  [the longest x1 6.17 us: body(): lax.all_to_all(outbox_terms.reshape(owners, capacity, block_width), 'blk'...]
    gather x3 -> x0, local copies, waits for them, and re-layouts: 7.19 us -> none  [the longest x1 3.04 us: body(): outgoing = latent[jnp.maximum(in_slots, 0)]]
    reduce_scatter x1 -> x0, waiting for transfers between devices: 6.13 us -> none  [body(): return lax.psum_scatter(stored, 'mc', scatter_dimension=1, tiled=True)]
    unnamed x10, local copies, waits for them, and re-layouts: 0.03 us -> 3.79 us
  transfers between devices with their start and end apart: 3 -> 1, of which waited for: 3 -> 1; matrix products, arithmetic and copies ran while one was open for 0% -> 0% of each run, Pallas kernels for 0% -> 0%
where the time goes in v1:
time: 108 us
  blocking collectives  75.8 us (70%)
  Pallas kernels  26.9 us (25%)
  local copies, waits for them, and re-layouts  3.79 us (4%)
    all_to_all x3, blocking collectives, swap(): lax.all_to_all(values, 'blk', split_axis=0, concat_axis=0, tiled=True)  75.8 us
    pallas_call x1, Pallas kernels, body(): pl.pallas_call(score_kernel, out_shape=jax.ShapeDtypeStruct((2, row_count...  12.5 us
    pallas_call x1, Pallas kernels, body(): pl.pallas_call(functools.partial(term_kernel, draws), out_shape=jax.Shape...  8.02 us
    unnamed x10, local copies, waits for them, and re-layouts  3.79 us
    pallas_call x1, Pallas kernels, body(): pl.pallas_call(gather_kernel, out_shape=jax.ShapeDtypeStruct((per_owner,...  2.56 us
    pallas_call x1, Pallas kernels, body(): pl.pallas_call(functools.partial(plan_kernel, owners, capacity, per_owner...  2.25 us
  transfers between devices with their start and end apart: 1, of which 1 were waited for; matrix products, arithmetic and copies ran while one was open for 0% of the time, Pallas kernels for 0%

profile of v1, /device:TPU:0, one launch (start us, length us, event | category | flops | bytes accessed | tf_op | source)
XLA Modules:
  0.0 107.9 jit_solution(14768859079790544920)
XLA Ops:
  0.0 2.3 %plan.1 = (s32[64,1,128]{2,1,0:T(1,128)}, s32[4,32]{1,0:T(4,128)}) custom-call(s32[1,32]{1,0:T(1,128)} %bitcast.7, s32[3,32]{1,0:T(4,128)} %bitcast.6, s32[128,128]{1,0:T(8,128)} %bitcast.5), custom_call_target="tpu_custom_call" | custom-call | tf_op jit(solution)/shard_map/plan/pallas_call | solution.py:149
  2.3 21.0 %all_to_all.15.slots_ref = s32[64,1,128]{2,1,0:T(1,128)S(1)} all-to-all(s32[64,1,128]{2,1,0:T(1,128)} %get-tuple-element.7), channel_id=1, replica_groups=mesh['blk'=64,'mc'=2] {'blk'}, dimensions={0} | all-to-all | bytes 65536 | tf_op jit(solution)/shard_map/all_to_all | solution.py:147
  23.2 0.0 copy-start.1
  23.2 1.6 %copy-done.1 = bf16[256,16,256]{2,1,0:T(8,128)(2,1)S(1)} copy-done((bf16[256,16,256]{2,1,0:T(8,128)(2,1)S(1)}, bf16[256,16,256]{2,1,0:T(8,128)(2,1)}, u32[]{:S(2)}) %copy-start.1) | copy-done | bytes 2097176
  24.8 0.0 copy-start.2
  24.8 1.7 %pack.1 = bf16[64,5,16,256]{3,2,1,0:T(8,128)(2,1)S(1)} custom-call(s32[64,1,128]{2,1,0:T(1,128)S(1)} %all_to_all.15.slots_ref, bf16[256,16,256]{2,1,0:T(8,128)(2,1)S(1)} %copy-done.1), custom_call_target="tpu_custom_call" | custom-call | tf_op jit(solution)/shard_map/pack/pallas_call | solution.py:160
  26.5 0.0 copy-start.4
  26.5 39.2 %all_to_all.16.fetched_ref = bf16[64,5,16,256]{3,2,1,0:T(8,128)(2,1)S(1)} all-to-all(bf16[64,5,16,256]{3,2,1,0:T(8,128)(2,1)S(1)} %pack.1), channel_id=1, replica_groups=mesh['blk'=64,'mc'=2] {'blk'}, dimensions={0} | all-to-all | bytes 5242880 | tf_op jit(solution)/shard_map/all_to_all | solution.py:147
  65.7 0.0 copy-done.2
  65.7 0.0 copy-done.4
  65.7 0.0 copy-start.3
  65.7 12.5 %score.1.mine_ref = f32[2,32,256]{2,1,0:T(8,128)S(1)} custom-call(s32[4,32]{1,0:T(4,128)S(1)} %copy-done.4, bf16[64,5,16,256]{3,2,1,0:T(8,128)(2,1)S(1)} %all_to_all.16.fetched_ref, bf16[32,256,256]{2,1,0:T(8,128)(2,1)} %diag_ref.3, bf16[32,3,256,256]{3,2,1,0:T(8,128)(2,1)} %cond_ref.3), custom_call_target="tpu_custom_call" | custom-call | tf_op jit(solution)/shard_map/score/pallas_call | solution.py:169
  78.1 0.1 collective-permute-start
  78.9 0.6 collective-permute-done.other_ref
  79.5 0.0 copy-done.3
  79.5 0.0 copy-start
  79.5 2.2 %copy-done = bf16[32,256,256]{2,1,0:T(8,128)(2,1)S(1)} copy-done((bf16[32,256,256]{2,1,0:T(8,128)(2,1)S(1)}, bf16[32,256,256]{2,1,0:T(8,128)(2,1)}, u32[]{:S(2)}) %copy-start) | copy-done | bytes 4194328
  81.6 8.0 %terms.1 = f32[64,5,128]{2,1,0:T(8,128)S(1)} custom-call(s32[4,32]{1,0:T(4,128)S(1)} %copy-done.4, f32[1,1]{1,0:T(1,128)} %bitcast.4.noise_ref, f32[2,32,256]{2,1,0:T(8,128)S(1)} %score.1.mine_ref, f32[2,32,256]{2,1,0:T(8,128)S(1)} %collective-permute-done.other_ref, f32[32,256]{1,0:T(8,128)S(1)} %copy-done.3, bf16[32,256,256]{2,1,0:T(8,128)(2,1)S(1)} %copy-done, ...), custom_call_target="tpu_custom_call" | custom-call | tf_op jit(solution)/shard_map/terms/pallas_call | solution.py:178
  89.7 15.6 %all_to_all.17.inbox_ref = f32[64,5,128]{2,1,0:T(8,128)} all-to-all(f32[64,5,128]{2,1,0:T(8,128)S(1)} %terms.1), channel_id=1, replica_groups=mesh['blk'=64,'mc'=2] {'blk'}, dimensions={0} | all-to-all | bytes 327680 | tf_op jit(solution)/shard_map/all_to_all | solution.py:147
  105.3 2.6 %collect.1 = f32[256,128]{1,0:T(8,128)} custom-call(s32[64,1,128]{2,1,0:T(1,128)} %copy-done.2, f32[64,5,128]{2,1,0:T(8,128)} %all_to_all.17.inbox_ref), custom_call_target="tpu_custom_call" | custom-call | tf_op jit(solution)/shard_map/collect/pallas_call | solution.py:188
Async XLA Ops:
  23.2 1.6 %copy-start.1 = (bf16[256,16,256]{2,1,0:T(8,128)(2,1)S(1)}, bf16[256,16,256]{2,1,0:T(8,128)(2,1)}, u32[]{:S(2)}) copy-start(bf16[256,16,256]{2,1,0:T(8,128)(2,1)} %latent_ref.1) | copy-start | bytes 6291460
  24.8 40.8 %copy-start.2 = (s32[64,1,128]{2,1,0:T(1,128)}, s32[64,1,128]{2,1,0:T(1,128)S(1)}, u32[]{:S(2)}) copy-start(s32[64,1,128]{2,1,0:T(1,128)S(1)} %all_to_all.15.slots_ref) | copy-start | bytes 98308
  26.5 39.2 %copy-start.4 = (s32[4,32]{1,0:T(4,128)S(1)}, s32[4,32]{1,0:T(4,128)}, u32[]{:S(2)}) copy-start(s32[4,32]{1,0:T(4,128)} %get-tuple-element.8.spot_ref) | copy-start | bytes 1540
  65.7 13.8 %copy-start.3 = (f32[32,256]{1,0:T(8,128)S(1)}, f32[32,256]{1,0:T(8,128)}, u32[]{:S(2)}) copy-start(f32[32,256]{1,0:T(8,128)} %obs_ref.1) | copy-start | bytes 98308
  78.1 1.3 %collective-permute-start = (f32[2,32,256]{2,1,0:T(8,128)S(1)}, f32[2,32,256]{2,1,0:T(8,128)S(1)}, u32[]{:S(2)}, u32[]{:S(2)}) collective-permute-start(f32[2,32,256]{2,1,0:T(8,128)S(1)} %score.1.mine_ref), channel_id=1, source_target_pairs={{0,1},{1,0},{2,3},{3,2},{4,5},{5,4},{6,7},{7,6},{8,9},{9,8},{10,11... | collective-permute-start | bytes 196616 | tf_op jit(solution)/shard_map/ppermute | solution.py:177
  79.5 2.2 %copy-start = (bf16[32,256,256]{2,1,0:T(8,128)(2,1)S(1)}, bf16[32,256,256]{2,1,0:T(8,128)(2,1)}, u32[]{:S(2)}) copy-start(bf16[32,256,256]{2,1,0:T(8,128)(2,1)} %diag_ref.3) | copy-start | bytes 12582916

commit v2 on v1

--- a/solution.py
+++ b/solution.py
@@ -10,11 +10,32 @@
 freedom = 4.0
 vmem = pl.BlockSpec(memory_space=pltpu.VMEM)
 smem = pl.BlockSpec(memory_space=pltpu.SMEM)
-budget = pltpu.CompilerParams(vmem_limit_bytes=48 * 1024 * 1024)
+anywhere = pl.BlockSpec(memory_space=pl.ANY)
 iota = lax.broadcasted_iota
 
 
-def plan_kernel(owners, capacity, per_owner, own_ref, near_ref, home_ref, outbox_ref, spot_ref):
+def budget(megabytes):
+    return pltpu.CompilerParams(vmem_limit_bytes=megabytes * 1024 * 1024)
+
+
+def in_hbm(values):
+    return pltpu.with_memory_space_constraint(values, pltpu.HBM)
+
+
+def plan_kernel(
+    owners, capacity, own_hbm, near_hbm, home_hbm, latent_hbm, outbox_ref, spot_ref, latent_ref, own_ref, near_ref, home_ref, sems
+):
+    per_owner = latent_ref.shape[0]
+    copies = [
+        pltpu.make_async_copy(home_hbm, home_ref, sems.at[0]),
+        pltpu.make_async_copy(own_hbm, own_ref, sems.at[1]),
+        pltpu.make_async_copy(near_hbm, near_ref, sems.at[2]),
+        pltpu.make_async_copy(latent_hbm, latent_ref, sems.at[3]),
+    ]
+    for copy in copies:
+        copy.start()
+    for copy in copies[:3]:
+        copy.wait()
     home = home_ref[...]
     high_count, low_count = home.shape
     dest_table = (home // per_owner).astype(jnp.float32).T.astype(jnp.bfloat16)
@@ -47,6 +68,7 @@
     for k in range(capacity):
         outbox = jnp.where(lanes == k, marks[k] - 1.0, outbox)
     outbox_ref[:, 0, :] = outbox.astype(jnp.int32)
+    copies[3].wait()
 
 
 def pack_kernel(slots_ref, latent_ref, out_ref):
@@ -60,12 +82,23 @@
     lax.fori_loop(0, owners, step, 0, unroll=4)
 
 
-def score_kernel(spot_ref, fetched_ref, diag_ref, cond_ref, sums_ref):
+def score_kernel(chunk, spot_ref, fetched_ref, diag_hbm, cond_hbm, sums_ref, diag_ref, cond_ref, sems):
     row_count, width = diag_ref.shape[:2]
     lower = iota(jnp.int32, (width, width), 0) >= iota(jnp.int32, (width, width), 1)
     turned = (((1,), (1,)), ((), ()))
 
-    def step(row, carry):
+    def copies(index):
+        part = pl.ds(index * chunk, chunk)
+        return (
+            pltpu.make_async_copy(diag_hbm.at[part], diag_ref.at[part], sems.at[0, index]),
+            pltpu.make_async_copy(cond_hbm.at[part], cond_ref.at[part], sems.at[1, index]),
+        )
+
+    for index in range(row_count // chunk):
+        for copy in copies(index):
+            copy.start()
+
+    def score(row):
         spots = [spot_ref[which, row] for which in range(1 + cond_ref.shape[1])]
         panels = [fetched_ref[spot // 8, spot % 8] for spot in spots]
         factor = jnp.where(lower, diag_ref[row], jnp.zeros((), diag_ref.dtype))
@@ -78,43 +111,67 @@
         scored = scored.astype(jnp.bfloat16).astype(jnp.float32)
         sums_ref[0, pl.ds(row, 1), :] = jnp.sum(scored, axis=0, keepdims=True)
         sums_ref[1, pl.ds(row, 1), :] = jnp.sum(panels[0].astype(jnp.float32), axis=0, keepdims=True)
+
+    def step(index, carry):
+        for copy in copies(index):
+            copy.wait()
+        for i in range(chunk):
+            score(index * chunk + i)
         return carry
 
-    lax.fori_loop(0, row_count, step, 0, unroll=2)
-
-
-def term_kernel(draws, spot_ref, noise_ref, mine_ref, other_ref, obs_ref, diag_ref, cond_ref, out_ref, likely_ref):
-    row_count, width = diag_ref.shape[:2]
-    half = out_ref.shape[2]
+    lax.fori_loop(0, row_count // chunk, step, 0)
+
+
+def term_kernel(
+    draws, chunk, spot_ref, noise_ref, mine_ref, other_ref, obs_ref, diag_hbm, cond_hbm, out_ref, likely_ref, diag_ref, cond_ref, sems
+):
+    row_count, width, half = diag_ref.shape
     first = pl.multiple_of(lax.axis_index("mc") * half, half)
+    columns = pl.ds(first, half)
+
+    def copies(index):
+        part = pl.ds(index * chunk, chunk)
+        return (
+            pltpu.make_async_copy(diag_hbm.at[part, :, columns], diag_ref.at[part], sems.at[0, index]),
+            pltpu.make_async_copy(cond_hbm.at[part, :, :, columns], cond_ref.at[part], sems.at[1, index]),
+        )
+
+    for index in range(row_count // chunk):
+        for copy in copies(index):
+            copy.start()
+
     lower = iota(jnp.int32, (width, half), 0) >= iota(jnp.int32, (width, half), 1) + first
     inverse_draws = 1.0 / draws
     which_row = iota(jnp.int32, (16, width), 0)
     out_ref[...] = jnp.zeros_like(out_ref)
-    part = pl.ds(first, half)
-    owned = mine_ref[1, :, part] + other_ref[1, :, part]
-    likely_ref[...] = noise_ref[0, 0] * (obs_ref[:, part] * float(draws) - owned)
-
-    def step(row, carry):
+    owned = mine_ref[1, :, columns] + other_ref[1, :, columns]
+    likely_ref[...] = noise_ref[0, 0] * (obs_ref[:, columns] * float(draws) - owned)
+
+    def term(row):
         total = mine_ref[0, pl.ds(row, 1), :] + other_ref[0, pl.ds(row, 1), :]
         coarse = total.astype(jnp.bfloat16).astype(jnp.float32)
         pieces = jnp.where(which_row == 0, coarse, jnp.where(which_row == 1, total - coarse, 0.0))
         pieces = pieces.astype(jnp.bfloat16)
-        likely = likely_ref[pl.ds(row, 1), :]
         for which in range(1 + cond_ref.shape[1]):
             if which == 0:
-                factor = diag_ref[row, :, part]
-                factor = jnp.where(lower, factor, jnp.zeros((), factor.dtype))
+                factor = jnp.where(lower, diag_ref[row], jnp.zeros((), diag_ref.dtype))
             else:
-                factor = cond_ref[row, which - 1, :, part]
+                factor = cond_ref[row, which - 1]
             back = jnp.dot(pieces, factor, preferred_element_type=jnp.float32)
-            back = jnp.sum(back, axis=0, keepdims=True)
-            term = (likely - back) * inverse_draws if which == 0 else -back * inverse_draws
+            back = back[0:1] + back[1:2]
+            if which == 0:
+                back = back - likely_ref[pl.ds(row, 1), :]
             spot = spot_ref[which, row]
-            out_ref[spot // 8, pl.ds(spot % 8, 1), :] = term
+            out_ref[spot // 8, pl.ds(spot % 8, 1), :] = back * -inverse_draws
+
+    def step(index, carry):
+        for copy in copies(index):
+            copy.wait()
+        for i in range(chunk):
+            term(index * chunk + i)
         return carry
 
-    lax.fori_loop(0, row_count, step, 0, unroll=2)
+    lax.fori_loop(0, row_count // chunk, step, 0)
 
 
 def gather_kernel(slots_ref, inbox_ref, out_ref):
@@ -146,42 +203,61 @@
     def swap(values):
         return lax.all_to_all(values, "blk", split_axis=0, concat_axis=0, tiled=True)
 
-    outbox, spot = pl.pallas_call(
-        functools.partial(plan_kernel, owners, capacity, per_owner),
+    outbox, spot, staged = pl.pallas_call(
+        functools.partial(plan_kernel, owners, capacity),
         out_shape=(
             jax.ShapeDtypeStruct((owners, 1, 128), jnp.int32),
             jax.ShapeDtypeStruct((want_kinds, row_count), jnp.int32),
+            pltpu.VMEM(latent.shape, latent.dtype),
         ),
-        in_specs=[vmem] * 3,
-        out_specs=(vmem, vmem),
+        in_specs=[anywhere] * 4,
+        out_specs=(vmem,) * 3,
+        scratch_shapes=[
+            pltpu.VMEM((1, row_count), jnp.int32),
+            pltpu.VMEM((want_kinds - 1, row_count), jnp.int32),
+            pltpu.VMEM((home.shape[0] // 128, 128), jnp.int32),
+            pltpu.SemaphoreType.DMA((4,)),
+        ],
+        compiler_params=budget(16),
         name="plan",
-    )(batch_ids.reshape(1, row_count), cond_ids.T, home.reshape(-1, 128))
+    )(in_hbm(batch_ids.reshape(1, row_count)), in_hbm(cond_ids.T), in_hbm(home.reshape(-1, 128)), in_hbm(latent))
     slots = swap(outbox)
     outgoing = pl.pallas_call(
         pack_kernel,
         out_shape=jax.ShapeDtypeStruct((owners, capacity, draw_count, width), latent.dtype),
         in_specs=[smem, vmem],
         out_specs=vmem,
-        compiler_params=budget,
+        compiler_params=budget(16),
         name="pack",
-    )(slots, latent)
+    )(slots, staged)
     fetched = swap(outgoing)
+    diag_factor, cond_factor, obs = in_hbm(diag_factor), in_hbm(cond_factor), in_hbm(obs)
     sums = pl.pallas_call(
-        score_kernel,
+        functools.partial(score_kernel, 8),
         out_shape=jax.ShapeDtypeStruct((2, row_count, width), jnp.float32),
-        in_specs=[smem, vmem, vmem, vmem],
-        out_specs=vmem,
-        compiler_params=budget,
+        in_specs=[smem, vmem, anywhere, anywhere],
+        out_specs=vmem,
+        scratch_shapes=[
+            pltpu.VMEM(diag_factor.shape, diag_factor.dtype),
+            pltpu.VMEM(cond_factor.shape, cond_factor.dtype),
+            pltpu.SemaphoreType.DMA((2, row_count // 8)),
+        ],
+        compiler_params=budget(32),
         name="score",
     )(spot, fetched, diag_factor, cond_factor)
     others = lax.ppermute(sums, "mc", [(0, 1), (1, 0)])
     terms = pl.pallas_call(
-        functools.partial(term_kernel, draws),
+        functools.partial(term_kernel, draws, 4),
         out_shape=jax.ShapeDtypeStruct((owners, capacity, half), jnp.float32),
-        in_specs=[smem, smem] + [vmem] * 5,
-        out_specs=vmem,
-        scratch_shapes=[pltpu.VMEM((row_count, half), jnp.float32)],
-        compiler_params=budget,
+        in_specs=[smem, smem, vmem, vmem, vmem, anywhere, anywhere],
+        out_specs=vmem,
+        scratch_shapes=[
+            pltpu.VMEM((row_count, half), jnp.float32),
+            pltpu.VMEM((row_count, width, half), diag_factor.dtype),
+            pltpu.VMEM((row_count, want_kinds - 1, width, half), cond_factor.dtype),
+            pltpu.SemaphoreType.DMA((2, row_count // 4)),
+        ],
+        compiler_params=budget(32),
         name="terms",
     )(spot, noise_prec.reshape(1, 1), sums, others, obs, diag_factor, cond_factor)
     inbox = swap(terms)
@@ -190,6 +266,7 @@
         out_shape=jax.ShapeDtypeStruct((per_owner, half), jnp.float32),
         in_specs=[vmem] * 2,
         out_specs=vmem,
+        compiler_params=budget(16),
         name="collect",
     )(slots, inbox)
 

time: 108 us -> 94.5 us (0.88)
  Pallas kernels: 26.9 us -> 17.4 us
  local copies, waits for them, and re-layouts: 3.79 us -> 0 us
    pallas_call x3, Pallas kernels: 22.7 us -> 14.1 us  [the longest x1 7.8 us: body(): pl.pallas_call(functools.partial(score_kernel, 8), out_shape=jax.ShapeDty...]
    unnamed x10 -> x0, local copies, waits for them, and re-layouts: 3.79 us -> none
where the time goes in v2:
time: 94.5 us; the launch traced here: 94.2 us
  blocking collectives  75.4 us (80%)
  Pallas kernels  17.4 us (18%)
    all_to_all x3, blocking collectives, swap(): lax.all_to_all(values, 'blk', split_axis=0, concat_axis=0, tiled=True)  75.4 us
    pallas_call x1, Pallas kernels, body(): pl.pallas_call(functools.partial(score_kernel, 8), out_shape=jax.ShapeDty...  7.8 us
    pallas_call x1, Pallas kernels, body(): pl.pallas_call(functools.partial(term_kernel, draws, 4), out_shape=jax.Sh...  4.65 us
  transfers between devices with their start and end apart: 1, of which 1 were waited for; matrix products, arithmetic and copies ran while one was open for 0% of the time, Pallas kernels for 0%

profile of v2, /device:TPU:0, one launch (start us, length us, event | category | flops | bytes accessed | tf_op | source)
XLA Modules:
  0.0 94.2 jit_solution(18298710990668569631)
XLA Ops:
  0.0 1.7 %plan.1 = (s32[64,1,128]{2,1,0:T(1,128)S(1)}, s32[4,32]{1,0:T(4,128)S(1)}, bf16[256,16,256]{2,1,0:T(8,128)(2,1)S(1)}) custom-call(s32[1,32]{1,0:T(1,128)} %bitcast.7, s32[3,32]{1,0:T(4,128)} %bitcast.6, s32[128,128]{1,0:T(8,128)} %bitcast.5, bf16[256,16,256]{2,1,0:T(8,128)(2,1)} %latent_hbm.1), custom_call_target="tpu_custom_call" | custom-call | tf_op jit(solution)/shard_map/plan/pallas_call | solution.py:206
  1.7 20.8 %all_to_all.15.slots_ref = s32[64,1,128]{2,1,0:T(1,128)S(1)} all-to-all(s32[64,1,128]{2,1,0:T(1,128)S(1)} %get-tuple-element.8), channel_id=1, replica_groups=mesh['blk'=64,'mc'=2] {'blk'}, dimensions={0} | all-to-all | bytes 65536 | tf_op jit(solution)/shard_map/all_to_all | solution.py:204
  22.6 1.7 %pack.1 = bf16[64,5,16,256]{3,2,1,0:T(8,128)(2,1)S(1)} custom-call(s32[64,1,128]{2,1,0:T(1,128)S(1)} %all_to_all.15.slots_ref, bf16[256,16,256]{2,1,0:T(8,128)(2,1)S(1)} %get-tuple-element.10.latent_ref), custom_call_target="tpu_custom_call" | custom-call | tf_op jit(solution)/shard_map/pack/pallas_call | solution.py:225
  24.2 39.2 %all_to_all.16.fetched_ref = bf16[64,5,16,256]{3,2,1,0:T(8,128)(2,1)S(1)} all-to-all(bf16[64,5,16,256]{3,2,1,0:T(8,128)(2,1)S(1)} %pack.1), channel_id=1, replica_groups=mesh['blk'=64,'mc'=2] {'blk'}, dimensions={0} | all-to-all | bytes 5242880 | tf_op jit(solution)/shard_map/all_to_all | solution.py:204
  63.4 7.8 %score.1.mine_ref = f32[2,32,256]{2,1,0:T(8,128)S(1)} custom-call(s32[4,32]{1,0:T(4,128)S(1)} %get-tuple-element.9.spot_ref, bf16[64,5,16,256]{3,2,1,0:T(8,128)(2,1)S(1)} %all_to_all.16.fetched_ref, bf16[32,256,256]{2,1,0:T(8,128)(2,1)} %diag_hbm.3, bf16[32,3,256,256]{3,2,1,0:T(8,128)(2,1)} %cond_hbm.3), custom_call_target="tpu_custom_call" | custom-call | tf_op jit(solution)/shard_map/score/pallas_call | solution.py:235
  71.2 0.1 collective-permute-start
  71.9 0.6 collective-permute-done.other_ref
  72.5 4.7 %terms.1 = f32[64,5,128]{2,1,0:T(8,128)S(1)} custom-call(s32[4,32]{1,0:T(4,128)S(1)} %get-tuple-element.9.spot_ref, f32[1,1]{1,0:T(1,128)} %bitcast.4.noise_ref, f32[2,32,256]{2,1,0:T(8,128)S(1)} %score.1.mine_ref, f32[2,32,256]{2,1,0:T(8,128)S(1)} %collective-permute-done.other_ref, f32[32,256]{1,0:T(8,128)} %obs_ref.1, bf16[32,256,256]{2,1,0:T(8,128)(2,1)} %diag_hbm.3, ...), custom_call_target="tpu_custom_call" | custom-call | tf_op jit(solution)/shard_map/terms/pallas_call | solution.py:249
  77.2 15.4 %all_to_all.17.inbox_ref = f32[64,5,128]{2,1,0:T(8,128)S(1)} all-to-all(f32[64,5,128]{2,1,0:T(8,128)S(1)} %terms.1), channel_id=1, replica_groups=mesh['blk'=64,'mc'=2] {'blk'}, dimensions={0} | all-to-all | bytes 327680 | tf_op jit(solution)/shard_map/all_to_all | solution.py:204
  92.6 1.6 %collect.1 = f32[256,128]{1,0:T(8,128)} custom-call(s32[64,1,128]{2,1,0:T(1,128)S(1)} %all_to_all.15.slots_ref, f32[64,5,128]{2,1,0:T(8,128)S(1)} %all_to_all.17.inbox_ref), custom_call_target="tpu_custom_call" | custom-call | tf_op jit(solution)/shard_map/collect/pallas_call | solution.py:264
Async XLA Ops:
  71.2 1.3 %collective-permute-start = (f32[2,32,256]{2,1,0:T(8,128)S(1)}, f32[2,32,256]{2,1,0:T(8,128)S(1)}, u32[]{:S(2)}, u32[]{:S(2)}) collective-permute-start(f32[2,32,256]{2,1,0:T(8,128)S(1)} %score.1.mine_ref), channel_id=1, source_target_pairs={{0,1},{1,0},{2,3},{3,2},{4,5},{5,4},{6,7},{7,6},{8,9},{9,8},{10,11... | collective-permute-start | bytes 196616 | tf_op jit(solution)/shard_map/ppermute | solution.py:248

commit v3 on v2

--- a/solution.py
+++ b/solution.py
@@ -22,8 +22,12 @@
     return pltpu.with_memory_space_constraint(values, pltpu.HBM)
 
 
+def in_vmem(values):
+    return pltpu.with_memory_space_constraint(values, pltpu.VMEM)
+
+
 def plan_kernel(
-    owners, capacity, own_hbm, near_hbm, home_hbm, latent_hbm, outbox_ref, spot_ref, latent_ref, own_ref, near_ref, home_ref, sems
+    owners, capacity, noise_ref, own_hbm, near_hbm, home_hbm, latent_hbm, outbox_ref, spot_ref, noise_row_ref, latent_ref, own_ref, near_ref, home_ref, sems
 ):
     per_owner = latent_ref.shape[0]
     copies = [
@@ -68,6 +72,7 @@
     for k in range(capacity):
         outbox = jnp.where(lanes == k, marks[k] - 1.0, outbox)
     outbox_ref[:, 0, :] = outbox.astype(jnp.int32)
+    noise_row_ref[...] = jnp.full(noise_row_ref.shape, noise_ref[0], jnp.float32)
     copies[3].wait()
 
 
@@ -82,26 +87,24 @@
     lax.fori_loop(0, owners, step, 0, unroll=4)
 
 
-def score_kernel(chunk, spot_ref, fetched_ref, diag_hbm, cond_hbm, sums_ref, diag_ref, cond_ref, sems):
+def score_kernel(
+    chunk, spot_ref, noise_ref, obs_ref, fetched_ref, diag_ref, cond_ref, sums_ref, diag_half_ref, cond_half_ref
+):
+    noise = noise_ref[...]
+    draw_count = float(fetched_ref.shape[2])
     row_count, width = diag_ref.shape[:2]
     lower = iota(jnp.int32, (width, width), 0) >= iota(jnp.int32, (width, width), 1)
     turned = (((1,), (1,)), ((), ()))
-
-    def copies(index):
-        part = pl.ds(index * chunk, chunk)
-        return (
-            pltpu.make_async_copy(diag_hbm.at[part], diag_ref.at[part], sems.at[0, index]),
-            pltpu.make_async_copy(cond_hbm.at[part], cond_ref.at[part], sems.at[1, index]),
-        )
-
-    for index in range(row_count // chunk):
-        for copy in copies(index):
-            copy.start()
+    half = diag_half_ref.shape[2]
+    columns = pl.ds(pl.multiple_of(lax.axis_index("mc") * half, half), half)
 
     def score(row):
         spots = [spot_ref[which, row] for which in range(1 + cond_ref.shape[1])]
         panels = [fetched_ref[spot // 8, spot % 8] for spot in spots]
         factor = jnp.where(lower, diag_ref[row], jnp.zeros((), diag_ref.dtype))
+        diag_half_ref[row] = diag_ref[row, :, columns]
+        for which in range(cond_ref.shape[1]):
+            cond_half_ref[row, which] = cond_ref[row, which, :, columns]
         whitened = lax.dot_general(panels[0], factor, turned, preferred_element_type=jnp.float32)
         for which in range(cond_ref.shape[1]):
             whitened = whitened + lax.dot_general(
@@ -110,11 +113,10 @@
         scored = (freedom + 1.0) * whitened / (freedom + whitened * whitened)
         scored = scored.astype(jnp.bfloat16).astype(jnp.float32)
         sums_ref[0, pl.ds(row, 1), :] = jnp.sum(scored, axis=0, keepdims=True)
-        sums_ref[1, pl.ds(row, 1), :] = jnp.sum(panels[0].astype(jnp.float32), axis=0, keepdims=True)
+        owned = jnp.sum(panels[0].astype(jnp.float32), axis=0, keepdims=True)
+        sums_ref[1, pl.ds(row, 1), :] = noise * (obs_ref[pl.ds(row, 1), :] * draw_count - owned)
 
     def step(index, carry):
-        for copy in copies(index):
-            copy.wait()
         for i in range(chunk):
             score(index * chunk + i)
         return carry
@@ -122,30 +124,16 @@
     lax.fori_loop(0, row_count // chunk, step, 0)
 
 
-def term_kernel(
-    draws, chunk, spot_ref, noise_ref, mine_ref, other_ref, obs_ref, diag_hbm, cond_hbm, out_ref, likely_ref, diag_ref, cond_ref, sems
-):
-    row_count, width, half = diag_ref.shape
+def term_kernel(draws, chunk, spot_ref, mine_ref, other_ref, diag_ref, cond_ref, out_ref, likely_ref):
+    row_count, width = diag_ref.shape[:2]
+    half = out_ref.shape[2]
     first = pl.multiple_of(lax.axis_index("mc") * half, half)
     columns = pl.ds(first, half)
-
-    def copies(index):
-        part = pl.ds(index * chunk, chunk)
-        return (
-            pltpu.make_async_copy(diag_hbm.at[part, :, columns], diag_ref.at[part], sems.at[0, index]),
-            pltpu.make_async_copy(cond_hbm.at[part, :, :, columns], cond_ref.at[part], sems.at[1, index]),
-        )
-
-    for index in range(row_count // chunk):
-        for copy in copies(index):
-            copy.start()
-
     lower = iota(jnp.int32, (width, half), 0) >= iota(jnp.int32, (width, half), 1) + first
     inverse_draws = 1.0 / draws
     which_row = iota(jnp.int32, (16, width), 0)
     out_ref[...] = jnp.zeros_like(out_ref)
-    owned = mine_ref[1, :, columns] + other_ref[1, :, columns]
-    likely_ref[...] = noise_ref[0, 0] * (obs_ref[:, columns] * float(draws) - owned)
+    likely_ref[...] = mine_ref[1, :, columns] + other_ref[1, :, columns]
 
     def term(row):
         total = mine_ref[0, pl.ds(row, 1), :] + other_ref[0, pl.ds(row, 1), :]
@@ -165,8 +153,6 @@
             out_ref[spot // 8, pl.ds(spot % 8, 1), :] = back * -inverse_draws
 
     def step(index, carry):
-        for copy in copies(index):
-            copy.wait()
         for i in range(chunk):
             term(index * chunk + i)
         return carry
@@ -203,15 +189,16 @@
     def swap(values):
         return lax.all_to_all(values, "blk", split_axis=0, concat_axis=0, tiled=True)
 
-    outbox, spot, staged = pl.pallas_call(
+    outbox, spot, noise_row, staged = pl.pallas_call(
         functools.partial(plan_kernel, owners, capacity),
         out_shape=(
             jax.ShapeDtypeStruct((owners, 1, 128), jnp.int32),
             jax.ShapeDtypeStruct((want_kinds, row_count), jnp.int32),
+            jax.ShapeDtypeStruct((1, width), jnp.float32),
             pltpu.VMEM(latent.shape, latent.dtype),
         ),
-        in_specs=[anywhere] * 4,
-        out_specs=(vmem,) * 3,
+        in_specs=[smem] + [anywhere] * 4,
+        out_specs=(vmem,) * 4,
         scratch_shapes=[
             pltpu.VMEM((1, row_count), jnp.int32),
             pltpu.VMEM((want_kinds - 1, row_count), jnp.int32),
@@ -220,46 +207,41 @@
         ],
         compiler_params=budget(16),
         name="plan",
-    )(in_hbm(batch_ids.reshape(1, row_count)), in_hbm(cond_ids.T), in_hbm(home.reshape(-1, 128)), in_hbm(latent))
+    )(noise_prec.reshape(1), in_hbm(batch_ids.reshape(1, row_count)), in_hbm(cond_ids.T), in_hbm(home.reshape(-1, 128)), in_hbm(latent))
     slots = swap(outbox)
     outgoing = pl.pallas_call(
         pack_kernel,
         out_shape=jax.ShapeDtypeStruct((owners, capacity, draw_count, width), latent.dtype),
         in_specs=[smem, vmem],
         out_specs=vmem,
-        compiler_params=budget(16),
+        compiler_params=budget(8),
+        cost_estimate=pl.CostEstimate(flops=10**11, transcendentals=0, bytes_accessed=10**8),
         name="pack",
     )(slots, staged)
     fetched = swap(outgoing)
-    diag_factor, cond_factor, obs = in_hbm(diag_factor), in_hbm(cond_factor), in_hbm(obs)
-    sums = pl.pallas_call(
+    diag_here, cond_here, obs = in_vmem(diag_factor), in_vmem(cond_factor), in_hbm(obs)
+    sums, diag_half, cond_half = pl.pallas_call(
         functools.partial(score_kernel, 8),
-        out_shape=jax.ShapeDtypeStruct((2, row_count, width), jnp.float32),
-        in_specs=[smem, vmem, anywhere, anywhere],
-        out_specs=vmem,
-        scratch_shapes=[
-            pltpu.VMEM(diag_factor.shape, diag_factor.dtype),
-            pltpu.VMEM(cond_factor.shape, cond_factor.dtype),
-            pltpu.SemaphoreType.DMA((2, row_count // 8)),
-        ],
-        compiler_params=budget(32),
+        out_shape=(
+            jax.ShapeDtypeStruct((2, row_count, width), jnp.float32),
+            jax.ShapeDtypeStruct((row_count, width, half), diag_factor.dtype),
+            jax.ShapeDtypeStruct((row_count, want_kinds - 1, width, half), cond_factor.dtype),
+        ),
+        in_specs=[smem] + [vmem] * 5,
+        out_specs=(vmem,) * 3,
+        compiler_params=budget(12),
         name="score",
-    )(spot, fetched, diag_factor, cond_factor)
+    )(spot, noise_row, obs, fetched, diag_here, cond_here)
     others = lax.ppermute(sums, "mc", [(0, 1), (1, 0)])
     terms = pl.pallas_call(
         functools.partial(term_kernel, draws, 4),
         out_shape=jax.ShapeDtypeStruct((owners, capacity, half), jnp.float32),
-        in_specs=[smem, smem, vmem, vmem, vmem, anywhere, anywhere],
+        in_specs=[smem] + [vmem] * 4,
         out_specs=vmem,
-        scratch_shapes=[
-            pltpu.VMEM((row_count, half), jnp.float32),
-            pltpu.VMEM((row_count, width, half), diag_factor.dtype),
-            pltpu.VMEM((row_count, want_kinds - 1, width, half), cond_factor.dtype),
-            pltpu.SemaphoreType.DMA((2, row_count // 4)),
-        ],
-        compiler_params=budget(32),
+        scratch_shapes=[pltpu.VMEM((row_count, half), jnp.float32)],
+        compiler_params=budget(12),
         name="terms",
-    )(spot, noise_prec.reshape(1, 1), sums, others, obs, diag_factor, cond_factor)
+    )(spot, sums, others, diag_half, cond_half)
     inbox = swap(terms)
     return pl.pallas_call(
         gather_kernel,

time: 94.5 us -> 92.9 us (0.983)
  Pallas kernels: 17.4 us -> 14.9 us
    pallas_call x1, Pallas kernels: 4.65 us -> 2.77 us  [body(): pl.pallas_call(functools.partial(term_kernel, draws, 4), out_shape=jax.Sh...]
where the time goes in v3:
time: 92.9 us; the launch traced here: 92.7 us
  blocking collectives  75.7 us (81%)
  Pallas kernels  14.9 us (16%)
  waiting for transfers between devices  1.24 us (1%)
    all_to_all x3, blocking collectives, swap(): lax.all_to_all(values, 'blk', split_axis=0, concat_axis=0, tiled=True)  75.7 us
    pallas_call x1, Pallas kernels, body(): pl.pallas_call(functools.partial(score_kernel, 8), out_shape=(jax.ShapeDt...  7.14 us
    pallas_call x1, Pallas kernels, body(): pl.pallas_call(functools.partial(term_kernel, draws, 4), out_shape=jax.Sh...  2.77 us
  transfers between devices with their start and end apart: 1, of which 1 were waited for; matrix products, arithmetic and copies ran while one was open for 0% of the time, Pallas kernels for 0%

profile of v3, /device:TPU:0, one launch (start us, length us, event | category | flops | bytes accessed | tf_op | source)
XLA Modules:
  0.0 92.7 jit_solution(2140415931564530346)
XLA Ops:
  0.7 1.7 %plan.1 = (s32[64,1,128]{2,1,0:T(1,128)S(1)}, s32[4,32]{1,0:T(4,128)S(1)}, f32[1,256]{1,0:T(1,128)S(1)}, bf16[256,16,256]{2,1,0:T(8,128)(2,1)S(1)}) custom-call(f32[1]{0:T(128)} %bitcast.4.noise_ref, s32[1,32]{1,0:T(1,128)} %bitcast.9, s32[3,32]{1,0:T(4,128)} %bitcast.8, s32[128,128]{1,0:T(8,128)} %bitcast.7, bf16[256,16,256]{2,1,0:T(8,128)(2,1)} %latent_hbm.1), custom_call_target="tpu_custom_call" | custom-call | tf_op jit(solution)/shard_map/plan/pallas_call | solution.py:192
  2.4 20.8 %all_to_all.15.slots_ref = s32[64,1,128]{2,1,0:T(1,128)S(1)} all-to-all(s32[64,1,128]{2,1,0:T(1,128)S(1)} %get-tuple-element.12), channel_id=1, replica_groups=mesh['blk'=64,'mc'=2] {'blk'}, dimensions={0} | all-to-all | bytes 65536 | tf_op jit(solution)/shard_map/all_to_all | solution.py:190
  23.2 0.0 slice-start
  23.2 0.0 slice-start.1
  23.2 0.0 slice-start.2
  23.2 1.7 %pack.1 = bf16[64,5,16,256]{3,2,1,0:T(8,128)(2,1)S(1)} custom-call(s32[64,1,128]{2,1,0:T(1,128)S(1)} %all_to_all.15.slots_ref, bf16[256,16,256]{2,1,0:T(8,128)(2,1)S(1)} %get-tuple-element.15.latent_ref), custom_call_target="tpu_custom_call" | custom-call | flops 99999997952 | bytes 100000000 | tf_op jit(solution)/shard_map/pack/pallas_call | solution.py:212
  24.9 0.0 copy-start
  24.9 39.4 %all_to_all.16.fetched_ref = bf16[64,5,16,256]{3,2,1,0:T(8,128)(2,1)S(1)} all-to-all(bf16[64,5,16,256]{3,2,1,0:T(8,128)(2,1)S(1)} %pack.1), channel_id=1, replica_groups=mesh['blk'=64,'mc'=2] {'blk'}, dimensions={0} | all-to-all | bytes 5242880 | tf_op jit(solution)/shard_map/all_to_all | solution.py:190
  64.3 0.0 slice-done
  64.3 0.0 slice-done.1
  64.3 0.0 slice-done.2
  64.3 0.0 copy-done
  64.3 7.1 %score.1 = (f32[2,32,256]{2,1,0:T(8,128)S(1)}, bf16[32,256,128]{2,1,0:T(8,128)(2,1)S(1)}, bf16[32,3,256,128]{3,2,1,0:T(8,128)(2,1)S(1)}) custom-call(s32[4,32]{1,0:T(4,128)S(1)} %get-tuple-element.13.spot_ref, f32[1,256]{1,0:T(1,128)S(1)} %get-tuple-element.14.noise_ref, f32[32,256]{1,0:T(8,128)} %obs_ref.1, ...), custom_call_target="tpu_custom_call" | custom-call | tf_op jit(solution)/shard_map/score/pallas_call | solution.py:223
  71.5 0.1 collective-permute-start
  71.6 1.2 %collective-permute-done.other_ref = f32[2,32,256]{2,1,0:T(8,128)S(1)} collective-permute-done((f32[2,32,256]{2,1,0:T(8,128)S(1)}, f32[2,32,256]{2,1,0:T(8,128)S(1)}, u32[]{:S(2)}, u32[]{:S(2)}) %collective-permute-start) | collective-permute-done | bytes 65568 | tf_op jit(solution)/shard_map/ppermute | solution.py:235
  72.8 2.8 %terms.1 = f32[64,5,128]{2,1,0:T(8,128)S(1)} custom-call(s32[4,32]{1,0:T(4,128)S(1)} %get-tuple-element.13.spot_ref, f32[2,32,256]{2,1,0:T(8,128)S(1)} %get-tuple-element.16.mine_ref, f32[2,32,256]{2,1,0:T(8,128)S(1)} %collective-permute-done.other_ref, bf16[32,256,128]{2,1,0:T(8,128)(2,1)S(1)} %get-tuple-element.17.diag_ref, ...), custom_call_target="tpu_custom_call" | custom-call | tf_op jit(solution)/shard_map/terms/pallas_call | solution.py:236
  75.6 15.5 %all_to_all.17.inbox_ref = f32[64,5,128]{2,1,0:T(8,128)S(1)} all-to-all(f32[64,5,128]{2,1,0:T(8,128)S(1)} %terms.1), channel_id=1, replica_groups=mesh['blk'=64,'mc'=2] {'blk'}, dimensions={0} | all-to-all | bytes 327680 | tf_op jit(solution)/shard_map/all_to_all | solution.py:190
  91.1 1.6 %collect.1 = f32[256,128]{1,0:T(8,128)} custom-call(s32[64,1,128]{2,1,0:T(1,128)S(1)} %all_to_all.15.slots_ref, f32[64,5,128]{2,1,0:T(8,128)S(1)} %all_to_all.17.inbox_ref), custom_call_target="tpu_custom_call" | custom-call | tf_op jit(solution)/shard_map/collect/pallas_call | solution.py:246
  (1 shorter events, 0.0 us)
Async XLA Ops:
  23.2 41.1 %slice-start = ((s8[12582912]{0:T(1024)(128)(4,1)}), s8[4194304]{0:T(1024)(128)(4,1)S(1)}, s32[]{:S(2)}) async-start(s8[12582912]{0:T(1024)(128)(4,1)} %bitcast.5), calls=%async_computation.3 | async-start | bytes 8388608
  23.2 41.1 %slice-start.1 = ((s8[12582912]{0:T(1024)(128)(4,1)}), s8[4194304]{0:T(1024)(128)(4,1)S(1)}, s32[]{:S(2)}) async-start(s8[12582912]{0:T(1024)(128)(4,1)} %bitcast.5), calls=%async_computation.4 | async-start | bytes 8388608
  23.2 41.1 %slice-start.2 = ((s8[12582912]{0:T(1024)(128)(4,1)}), s8[4194304]{0:T(1024)(128)(4,1)S(1)}, s32[]{:S(2)}) async-start(s8[12582912]{0:T(1024)(128)(4,1)} %bitcast.5), calls=%async_computation.5 | async-start | bytes 8388608
  24.9 39.5 %copy-start = (bf16[32,256,256]{2,1,0:T(8,128)(2,1)S(1)}, bf16[32,256,256]{2,1,0:T(8,128)(2,1)}, u32[]{:S(2)}) copy-start(bf16[32,256,256]{2,1,0:T(8,128)(2,1)} %diag_ref.1) | copy-start | bytes 12582916
  71.5 1.3 %collective-permute-start = (f32[2,32,256]{2,1,0:T(8,128)S(1)}, f32[2,32,256]{2,1,0:T(8,128)S(1)}, u32[]{:S(2)}, u32[]{:S(2)}) collective-permute-start(f32[2,32,256]{2,1,0:T(8,128)S(1)} %get-tuple-element.16.mine_ref), channel_id=1, source_target_pairs={{0,1},{1,0},{2,3},{3,2},{4,5},{5,4},{6,7},{7,6},{8,9},{9,8},{10,11... | collective-permute-start | bytes 196616 | tf_op jit(solution)/shard_map/ppermute | solution.py:235

commit v4 on v3

--- a/solution.py
+++ b/solution.py
@@ -76,36 +76,36 @@
     copies[3].wait()
 
 
-def pack_kernel(slots_ref, latent_ref, out_ref):
+def pack_kernel(slots_ref, latent_ref, out_ref, turned_ref, scalar_ref, sem):
     owners, capacity = out_ref.shape[:2]
+    turned = jnp.maximum(slots_ref[:, 0, :], 0).astype(jnp.float32).T
+    turned_ref[:, pl.ds(0, owners)] = turned[: turned_ref.shape[0]].astype(jnp.int32)
+    copy = pltpu.make_async_copy(turned_ref, scalar_ref, sem)
+    copy.start()
+    copy.wait()
 
     def step(dev, carry):
         for k in range(capacity):
-            out_ref[dev, k] = latent_ref[jnp.maximum(slots_ref[dev, 0, k], 0)]
+            out_ref[dev, k] = latent_ref[scalar_ref[k, dev]]
         return carry
 
-    lax.fori_loop(0, owners, step, 0, unroll=4)
+    lax.fori_loop(0, owners, step, 0, unroll=8)
 
 
 def score_kernel(
-    chunk, spot_ref, noise_ref, obs_ref, fetched_ref, diag_ref, cond_ref, sums_ref, diag_half_ref, cond_half_ref
+    chunk, spot_ref, noise_ref, obs_ref, fetched_ref, diag_ref, cond_ref, sums_ref
 ):
     noise = noise_ref[...]
     draw_count = float(fetched_ref.shape[2])
     row_count, width = diag_ref.shape[:2]
     lower = iota(jnp.int32, (width, width), 0) >= iota(jnp.int32, (width, width), 1)
     turned = (((1,), (1,)), ((), ()))
-    half = diag_half_ref.shape[2]
-    columns = pl.ds(pl.multiple_of(lax.axis_index("mc") * half, half), half)
 
     def score(row):
         spots = [spot_ref[which, row] for which in range(1 + cond_ref.shape[1])]
         panels = [fetched_ref[spot // 8, spot % 8] for spot in spots]
         factor = jnp.where(lower, diag_ref[row], jnp.zeros((), diag_ref.dtype))
-        diag_half_ref[row] = diag_ref[row, :, columns]
-        for which in range(cond_ref.shape[1]):
-            cond_half_ref[row, which] = cond_ref[row, which, :, columns]
-        whitened = lax.dot_general(panels[0], factor, turned, preferred_element_type=jnp.float32)
+        whitened = lax.dot_general(factor, panels[0], turned, preferred_element_type=jnp.float32).T
         for which in range(cond_ref.shape[1]):
             whitened = whitened + lax.dot_general(
                 panels[which + 1], cond_ref[row, which], turned, preferred_element_type=jnp.float32
@@ -142,9 +142,9 @@
         pieces = pieces.astype(jnp.bfloat16)
         for which in range(1 + cond_ref.shape[1]):
             if which == 0:
-                factor = jnp.where(lower, diag_ref[row], jnp.zeros((), diag_ref.dtype))
+                factor = jnp.where(lower, diag_ref[row, :, columns], jnp.zeros((), diag_ref.dtype))
             else:
-                factor = cond_ref[row, which - 1]
+                factor = cond_ref[row, which - 1, :, columns]
             back = jnp.dot(pieces, factor, preferred_element_type=jnp.float32)
             back = back[0:1] + back[1:2]
             if which == 0:
@@ -164,15 +164,15 @@
     owners, capacity, half = inbox_ref.shape
     per_owner = out_ref.shape[0]
     slots = slots_ref[:, 0, :].astype(jnp.float32).T
-    places = iota(jnp.int32, (per_owner, owners), 0).astype(jnp.float32)
+    slots = jnp.concatenate([slots[k : k + 1, :] for k in range(capacity)], axis=1)
+    places = iota(jnp.int32, (per_owner, owners * capacity), 0).astype(jnp.float32)
+    hot = (places == slots).astype(jnp.bfloat16)
+    rest = jnp.concatenate([inbox_ref[:, k, :] for k in range(capacity)], axis=0)
     total = jnp.zeros((per_owner, half), jnp.float32)
-    for k in range(capacity):
-        hot = (places == slots[k : k + 1, :]).astype(jnp.bfloat16)
-        rest = inbox_ref[:, k, :]
-        for _ in range(3):
-            piece = rest.astype(jnp.bfloat16)
-            rest = rest - piece.astype(jnp.float32)
-            total = total + jnp.dot(hot, piece, preferred_element_type=jnp.float32)
+    for _ in range(3):
+        piece = rest.astype(jnp.bfloat16)
+        rest = rest - piece.astype(jnp.float32)
+        total = total + jnp.dot(hot, piece, preferred_element_type=jnp.float32)
     out_ref[...] = total
 
 
@@ -212,36 +212,37 @@
     outgoing = pl.pallas_call(
         pack_kernel,
         out_shape=jax.ShapeDtypeStruct((owners, capacity, draw_count, width), latent.dtype),
-        in_specs=[smem, vmem],
-        out_specs=vmem,
+        in_specs=[vmem, vmem],
+        out_specs=vmem,
+        scratch_shapes=[
+            pltpu.VMEM((8, 128), jnp.int32),
+            pltpu.SMEM((8, 128), jnp.int32),
+            pltpu.SemaphoreType.DMA,
+        ],
         compiler_params=budget(8),
         cost_estimate=pl.CostEstimate(flops=10**11, transcendentals=0, bytes_accessed=10**8),
         name="pack",
     )(slots, staged)
     fetched = swap(outgoing)
     diag_here, cond_here, obs = in_vmem(diag_factor), in_vmem(cond_factor), in_hbm(obs)
-    sums, diag_half, cond_half = pl.pallas_call(
-        functools.partial(score_kernel, 8),
-        out_shape=(
-            jax.ShapeDtypeStruct((2, row_count, width), jnp.float32),
-            jax.ShapeDtypeStruct((row_count, width, half), diag_factor.dtype),
-            jax.ShapeDtypeStruct((row_count, want_kinds - 1, width, half), cond_factor.dtype),
-        ),
+    sums = pl.pallas_call(
+        functools.partial(score_kernel, 16),
+        out_shape=jax.ShapeDtypeStruct((2, row_count, width), jnp.float32),
         in_specs=[smem] + [vmem] * 5,
-        out_specs=(vmem,) * 3,
+        out_specs=vmem,
         compiler_params=budget(12),
         name="score",
     )(spot, noise_row, obs, fetched, diag_here, cond_here)
     others = lax.ppermute(sums, "mc", [(0, 1), (1, 0)])
     terms = pl.pallas_call(
-        functools.partial(term_kernel, draws, 4),
+        functools.partial(term_kernel, draws, 8),
         out_shape=jax.ShapeDtypeStruct((owners, capacity, half), jnp.float32),
         in_specs=[smem] + [vmem] * 4,
         out_specs=vmem,
         scratch_shapes=[pltpu.VMEM((row_count, half), jnp.float32)],
         compiler_params=budget(12),
         name="terms",
-    )(spot, sums, others, diag_half, cond_half)
+    )(spot, sums, others, diag_here, cond_here)
     inbox = swap(terms)
     return pl.pallas_call(
         gather_kernel,

time: 92.9 us -> 89.3 us (0.961)
  Pallas kernels: 14.9 us -> 11.2 us
    pallas_call x2, Pallas kernels: 9.92 us -> 7.23 us  [the longest x1 4.75 us: body(): pl.pallas_call(functools.partial(score_kernel, 16), out_shape=jax.ShapeDt...]
where the time goes in v4:
time: 89.3 us; the launch traced here: 89 us
  blocking collectives  75.7 us (85%)
  Pallas kernels  11.2 us (13%)
  waiting for transfers between devices  1.24 us (1%)
    all_to_all x3, blocking collectives, swap(): lax.all_to_all(values, 'blk', split_axis=0, concat_axis=0, tiled=True)  75.7 us
    pallas_call x1, Pallas kernels, body(): pl.pallas_call(functools.partial(score_kernel, 16), out_shape=jax.ShapeDt...  4.75 us
    pallas_call x1, Pallas kernels, body(): pl.pallas_call(functools.partial(term_kernel, draws, 8), out_shape=jax.Sh...  2.49 us
  transfers between devices with their start and end apart: 1, of which 1 were waited for; matrix products, arithmetic and copies ran while one was open for 0% of the time, Pallas kernels for 0%

profile of v4, /device:TPU:0, one launch (start us, length us, event | category | flops | bytes accessed | tf_op | source)
XLA Modules:
  0.0 89.0 jit_solution(16414214673603899909)
XLA Ops:
  0.7 1.7 %plan.1 = (s32[64,1,128]{2,1,0:T(1,128)S(1)}, s32[4,32]{1,0:T(4,128)S(1)}, f32[1,256]{1,0:T(1,128)S(1)}, bf16[256,16,256]{2,1,0:T(8,128)(2,1)S(1)}) custom-call(f32[1]{0:T(128)} %bitcast.4.noise_ref, s32[1,32]{1,0:T(1,128)} %bitcast.9, s32[3,32]{1,0:T(4,128)} %bitcast.8, s32[128,128]{1,0:T(8,128)} %bitcast.7, bf16[256,16,256]{2,1,0:T(8,128)(2,1)} %latent_hbm.1), custom_call_target="tpu_custom_call" | custom-call | tf_op jit(solution)/shard_map/plan/pallas_call | solution.py:192
  2.4 20.8 %all_to_all.15.slots_ref = s32[64,1,128]{2,1,0:T(1,128)S(1)} all-to-all(s32[64,1,128]{2,1,0:T(1,128)S(1)} %get-tuple-element.9), channel_id=1, replica_groups=mesh['blk'=64,'mc'=2] {'blk'}, dimensions={0} | all-to-all | bytes 65536 | tf_op jit(solution)/shard_map/all_to_all | solution.py:190
  23.2 0.0 slice-start
  23.2 0.0 slice-start.1
  23.2 0.0 slice-start.2
  23.2 1.2 %pack.1 = bf16[64,5,16,256]{3,2,1,0:T(8,128)(2,1)S(1)} custom-call(s32[64,1,128]{2,1,0:T(1,128)S(1)} %all_to_all.15.slots_ref, bf16[256,16,256]{2,1,0:T(8,128)(2,1)S(1)} %get-tuple-element.12.latent_ref), custom_call_target="tpu_custom_call" | custom-call | flops 99999997952 | bytes 100000000 | tf_op jit(solution)/shard_map/pack/pallas_call | solution.py:212
  24.4 0.0 copy-start
  24.4 39.4 %all_to_all.16.fetched_ref = bf16[64,5,16,256]{3,2,1,0:T(8,128)(2,1)S(1)} all-to-all(bf16[64,5,16,256]{3,2,1,0:T(8,128)(2,1)S(1)} %pack.1), channel_id=1, replica_groups=mesh['blk'=64,'mc'=2] {'blk'}, dimensions={0} | all-to-all | bytes 5242880 | tf_op jit(solution)/shard_map/all_to_all | solution.py:190
  63.9 0.0 slice-done
  63.9 0.0 slice-done.1
  63.9 0.0 slice-done.2
  63.9 0.0 copy-done
  63.9 4.7 %score.1.mine_ref = f32[2,32,256]{2,1,0:T(8,128)S(1)} custom-call(s32[4,32]{1,0:T(4,128)S(1)} %get-tuple-element.10.spot_ref, f32[1,256]{1,0:T(1,128)S(1)} %get-tuple-element.11.noise_ref, f32[32,256]{1,0:T(8,128)} %obs_ref.1, bf16[64,5,16,256]{3,2,1,0:T(8,128)(2,1)S(1)} %all_to_all.16.fetched_ref, bf16[32,256,256]{2,1,0:T(8,128)(2,1)S(1)} %copy-done, ...), custom_call_target="tpu_custom_call" | custom-call | tf_op jit(solution)/shard_map/score/pallas_call | solution.py:228
  68.6 0.1 collective-permute-start
  68.7 1.2 %collective-permute-done.other_ref = f32[2,32,256]{2,1,0:T(8,128)S(1)} collective-permute-done((f32[2,32,256]{2,1,0:T(8,128)S(1)}, f32[2,32,256]{2,1,0:T(8,128)S(1)}, u32[]{:S(2)}, u32[]{:S(2)}) %collective-permute-start) | collective-permute-done | bytes 65568 | tf_op jit(solution)/shard_map/ppermute | solution.py:236
  70.0 2.5 %terms.1 = f32[64,5,128]{2,1,0:T(8,128)S(1)} custom-call(s32[4,32]{1,0:T(4,128)S(1)} %get-tuple-element.10.spot_ref, f32[2,32,256]{2,1,0:T(8,128)S(1)} %score.1.mine_ref, f32[2,32,256]{2,1,0:T(8,128)S(1)} %collective-permute-done.other_ref, bf16[32,256,256]{2,1,0:T(8,128)(2,1)S(1)} %copy-done, bf16[32,3,256,256]{3,2,1,0:T(8,128)(2,1)S(1)} %bitcast.6), custom_call_target="tpu_custom_call" | custom-call | tf_op jit(solution)/shard_map/terms/pallas_call | solution.py:237
  72.5 15.5 %all_to_all.17.inbox_ref = f32[64,5,128]{2,1,0:T(8,128)S(1)} all-to-all(f32[64,5,128]{2,1,0:T(8,128)S(1)} %terms.1), channel_id=1, replica_groups=mesh['blk'=64,'mc'=2] {'blk'}, dimensions={0} | all-to-all | bytes 327680 | tf_op jit(solution)/shard_map/all_to_all | solution.py:190
  87.9 1.1 %collect.1 = f32[256,128]{1,0:T(8,128)} custom-call(s32[64,1,128]{2,1,0:T(1,128)S(1)} %all_to_all.15.slots_ref, f32[64,5,128]{2,1,0:T(8,128)S(1)} %all_to_all.17.inbox_ref), custom_call_target="tpu_custom_call" | custom-call | tf_op jit(solution)/shard_map/collect/pallas_call | solution.py:247
  (1 shorter events, 0.0 us)
Async XLA Ops:
  23.2 40.6 %slice-start = ((s8[12582912]{0:T(1024)(128)(4,1)}), s8[4194304]{0:T(1024)(128)(4,1)S(1)}, s32[]{:S(2)}) async-start(s8[12582912]{0:T(1024)(128)(4,1)} %bitcast.5), calls=%async_computation.3 | async-start | bytes 8388608
  23.2 40.6 %slice-start.1 = ((s8[12582912]{0:T(1024)(128)(4,1)}), s8[4194304]{0:T(1024)(128)(4,1)S(1)}, s32[]{:S(2)}) async-start(s8[12582912]{0:T(1024)(128)(4,1)} %bitcast.5), calls=%async_computation.4 | async-start | bytes 8388608
  23.2 40.6 %slice-start.2 = ((s8[12582912]{0:T(1024)(128)(4,1)}), s8[4194304]{0:T(1024)(128)(4,1)S(1)}, s32[]{:S(2)}) async-start(s8[12582912]{0:T(1024)(128)(4,1)} %bitcast.5), calls=%async_computation.5 | async-start | bytes 8388608
  24.4 39.5 %copy-start = (bf16[32,256,256]{2,1,0:T(8,128)(2,1)S(1)}, bf16[32,256,256]{2,1,0:T(8,128)(2,1)}, u32[]{:S(2)}) copy-start(bf16[32,256,256]{2,1,0:T(8,128)(2,1)} %diag_ref.3) | copy-start | bytes 12582916
  68.6 1.3 %collective-permute-start = (f32[2,32,256]{2,1,0:T(8,128)S(1)}, f32[2,32,256]{2,1,0:T(8,128)S(1)}, u32[]{:S(2)}, u32[]{:S(2)}) collective-permute-start(f32[2,32,256]{2,1,0:T(8,128)S(1)} %score.1.mine_ref), channel_id=1, source_target_pairs={{0,1},{1,0},{2,3},{3,2},{4,5},{5,4},{6,7},{7,6},{8,9},{9,8},{10,11... | collective-permute-start | bytes 196616 | tf_op jit(solution)/shard_map/ppermute | solution.py:236

commit v5 on v4

--- a/solution.py
+++ b/solution.py
@@ -100,13 +100,17 @@
     row_count, width = diag_ref.shape[:2]
     lower = iota(jnp.int32, (width, width), 0) >= iota(jnp.int32, (width, width), 1)
     turned = (((1,), (1,)), ((), ()))
+    cut = width // 2
 
     def score(row):
         spots = [spot_ref[which, row] for which in range(1 + cond_ref.shape[1])]
         panels = [fetched_ref[spot // 8, spot % 8] for spot in spots]
         factor = jnp.where(lower, diag_ref[row], jnp.zeros((), diag_ref.dtype))
         whitened = lax.dot_general(factor, panels[0], turned, preferred_element_type=jnp.float32).T
-        for which in range(cond_ref.shape[1]):
+        top = lax.dot_general(cond_ref[row, 0, pl.ds(0, cut)], panels[1], turned, preferred_element_type=jnp.float32).T
+        low = lax.dot_general(panels[1], cond_ref[row, 0, pl.ds(cut, cut)], turned, preferred_element_type=jnp.float32)
+        whitened = whitened + jnp.concatenate([top, low], axis=1)
+        for which in range(1, cond_ref.shape[1]):
             whitened = whitened + lax.dot_general(
                 panels[which + 1], cond_ref[row, which], turned, preferred_element_type=jnp.float32
             )
@@ -126,7 +130,7 @@
 
 def term_kernel(draws, chunk, spot_ref, mine_ref, other_ref, diag_ref, cond_ref, out_ref, likely_ref):
     row_count, width = diag_ref.shape[:2]
-    half = out_ref.shape[2]
+    half = likely_ref.shape[1]
     first = pl.multiple_of(lax.axis_index("mc") * half, half)
     columns = pl.ds(first, half)
     lower = iota(jnp.int32, (width, half), 0) >= iota(jnp.int32, (width, half), 1) + first
@@ -150,7 +154,8 @@
             if which == 0:
                 back = back - likely_ref[pl.ds(row, 1), :]
             spot = spot_ref[which, row]
-            out_ref[spot // 8, pl.ds(spot % 8, 1), :] = back * -inverse_draws
+            place = pl.multiple_of((spot % 8) * half, half)
+            out_ref[spot // 8, :, pl.ds(place, half)] = back * -inverse_draws
 
     def step(index, carry):
         for i in range(chunk):
@@ -161,13 +166,14 @@
 
 
 def gather_kernel(slots_ref, inbox_ref, out_ref):
-    owners, capacity, half = inbox_ref.shape
-    per_owner = out_ref.shape[0]
+    owners = inbox_ref.shape[0]
+    per_owner, half = out_ref.shape
+    capacity = inbox_ref.shape[2] // half
     slots = slots_ref[:, 0, :].astype(jnp.float32).T
     slots = jnp.concatenate([slots[k : k + 1, :] for k in range(capacity)], axis=1)
     places = iota(jnp.int32, (per_owner, owners * capacity), 0).astype(jnp.float32)
     hot = (places == slots).astype(jnp.bfloat16)
-    rest = jnp.concatenate([inbox_ref[:, k, :] for k in range(capacity)], axis=0)
+    rest = jnp.concatenate([inbox_ref[:, 0, pl.ds(k * half, half)] for k in range(capacity)], axis=0)
     total = jnp.zeros((per_owner, half), jnp.float32)
     for _ in range(3):
         piece = rest.astype(jnp.bfloat16)
@@ -226,7 +232,7 @@
     fetched = swap(outgoing)
     diag_here, cond_here, obs = in_vmem(diag_factor), in_vmem(cond_factor), in_hbm(obs)
     sums = pl.pallas_call(
-        functools.partial(score_kernel, 16),
+        functools.partial(score_kernel, 32),
         out_shape=jax.ShapeDtypeStruct((2, row_count, width), jnp.float32),
         in_specs=[smem] + [vmem] * 5,
         out_specs=vmem,
@@ -235,8 +241,8 @@
     )(spot, noise_row, obs, fetched, diag_here, cond_here)
     others = lax.ppermute(sums, "mc", [(0, 1), (1, 0)])
     terms = pl.pallas_call(
-        functools.partial(term_kernel, draws, 8),
-        out_shape=jax.ShapeDtypeStruct((owners, capacity, half), jnp.float32),
+        functools.partial(term_kernel, draws, 32),
+        out_shape=jax.ShapeDtypeStruct((owners, 1, capacity * half), jnp.float32),
         in_specs=[smem] + [vmem] * 4,
         out_specs=vmem,
         scratch_shapes=[pltpu.VMEM((row_count, half), jnp.float32)],

time: 89.3 us -> 87.7 us (0.982)
  no operation moved by 1% of the time
where the time goes in v5:
time: 87.7 us; the launch traced here: 87.5 us
  blocking collectives  74.9 us (85%)
  Pallas kernels  10.5 us (12%)
  waiting for transfers between devices  1.24 us (1%)
    all_to_all x3, blocking collectives, swap(): lax.all_to_all(values, 'blk', split_axis=0, concat_axis=0, tiled=True)  74.9 us
    pallas_call x1, Pallas kernels, body(): pl.pallas_call(functools.partial(score_kernel, 32), out_shape=jax.ShapeDt...  4.41 us
    pallas_call x1, Pallas kernels, body(): pl.pallas_call(functools.partial(term_kernel, draws, 32), out_shape=jax.S...  2.08 us
  transfers between devices with their start and end apart: 1, of which 1 were waited for; matrix products, arithmetic and copies ran while one was open for 0% of the time, Pallas kernels for 0%

profile of v5, /device:TPU:0, one launch (start us, length us, event | category | flops | bytes accessed | tf_op | source)
XLA Modules:
  0.0 87.5 jit_solution(2820078091566194117)
XLA Ops:
  0.7 1.7 %plan.1 = (s32[64,1,128]{2,1,0:T(1,128)S(1)}, s32[4,32]{1,0:T(4,128)S(1)}, f32[1,256]{1,0:T(1,128)S(1)}, bf16[256,16,256]{2,1,0:T(8,128)(2,1)S(1)}) custom-call(f32[1]{0:T(128)} %bitcast.4.noise_ref, s32[1,32]{1,0:T(1,128)} %bitcast.9, s32[3,32]{1,0:T(4,128)} %bitcast.8, s32[128,128]{1,0:T(8,128)} %bitcast.7, bf16[256,16,256]{2,1,0:T(8,128)(2,1)} %latent_hbm.1), custom_call_target="tpu_custom_call" | custom-call | tf_op jit(solution)/shard_map/plan/pallas_call | solution.py:198
  2.4 20.8 %all_to_all.15.slots_ref = s32[64,1,128]{2,1,0:T(1,128)S(1)} all-to-all(s32[64,1,128]{2,1,0:T(1,128)S(1)} %get-tuple-element.9), channel_id=1, replica_groups=mesh['blk'=64,'mc'=2] {'blk'}, dimensions={0} | all-to-all | bytes 65536 | tf_op jit(solution)/shard_map/all_to_all | solution.py:196
  23.2 0.0 slice-start
  23.2 0.0 slice-start.1
  23.2 0.0 slice-start.2
  23.2 1.2 %pack.1 = bf16[64,5,16,256]{3,2,1,0:T(8,128)(2,1)S(1)} custom-call(s32[64,1,128]{2,1,0:T(1,128)S(1)} %all_to_all.15.slots_ref, bf16[256,16,256]{2,1,0:T(8,128)(2,1)S(1)} %get-tuple-element.12.latent_ref), custom_call_target="tpu_custom_call" | custom-call | flops 99999997952 | bytes 100000000 | tf_op jit(solution)/shard_map/pack/pallas_call | solution.py:218
  24.4 0.0 copy-start
  24.4 39.4 %all_to_all.16.fetched_ref = bf16[64,5,16,256]{3,2,1,0:T(8,128)(2,1)S(1)} all-to-all(bf16[64,5,16,256]{3,2,1,0:T(8,128)(2,1)S(1)} %pack.1), channel_id=1, replica_groups=mesh['blk'=64,'mc'=2] {'blk'}, dimensions={0} | all-to-all | bytes 5242880 | tf_op jit(solution)/shard_map/all_to_all | solution.py:196
  63.9 0.0 slice-done
  63.9 0.0 slice-done.1
  63.9 0.0 slice-done.2
  63.9 0.0 copy-done
  63.9 4.4 %score.1.mine_ref = f32[2,32,256]{2,1,0:T(8,128)S(1)} custom-call(s32[4,32]{1,0:T(4,128)S(1)} %get-tuple-element.10.spot_ref, f32[1,256]{1,0:T(1,128)S(1)} %get-tuple-element.11.noise_ref, f32[32,256]{1,0:T(8,128)} %obs_ref.1, bf16[64,5,16,256]{3,2,1,0:T(8,128)(2,1)S(1)} %all_to_all.16.fetched_ref, bf16[32,256,256]{2,1,0:T(8,128)(2,1)S(1)} %copy-done, ...), custom_call_target="tpu_custom_call" | custom-call | tf_op jit(solution)/shard_map/score/pallas_call | solution.py:234
  68.3 0.1 collective-permute-start
  68.4 1.2 %collective-permute-done.other_ref = f32[2,32,256]{2,1,0:T(8,128)S(1)} collective-permute-done((f32[2,32,256]{2,1,0:T(8,128)S(1)}, f32[2,32,256]{2,1,0:T(8,128)S(1)}, u32[]{:S(2)}, u32[]{:S(2)}) %collective-permute-start) | collective-permute-done | bytes 65568 | tf_op jit(solution)/shard_map/ppermute | solution.py:242
  69.6 2.1 %terms.1 = f32[64,1,640]{2,1,0:T(1,128)S(1)} custom-call(s32[4,32]{1,0:T(4,128)S(1)} %get-tuple-element.10.spot_ref, f32[2,32,256]{2,1,0:T(8,128)S(1)} %score.1.mine_ref, f32[2,32,256]{2,1,0:T(8,128)S(1)} %collective-permute-done.other_ref, bf16[32,256,256]{2,1,0:T(8,128)(2,1)S(1)} %copy-done, bf16[32,3,256,256]{3,2,1,0:T(8,128)(2,1)S(1)} %bitcast.6), custom_call_target="tpu_custom_call" | custom-call | tf_op jit(solution)/shard_map/terms/pallas_call | solution.py:243
  71.7 14.7 %all_to_all.17.inbox_ref = f32[64,1,640]{2,1,0:T(1,128)S(1)} all-to-all(f32[64,1,640]{2,1,0:T(1,128)S(1)} %terms.1), channel_id=1, replica_groups=mesh['blk'=64,'mc'=2] {'blk'}, dimensions={0} | all-to-all | bytes 327680 | tf_op jit(solution)/shard_map/all_to_all | solution.py:196
  86.4 1.1 %collect.1 = f32[256,128]{1,0:T(8,128)} custom-call(s32[64,1,128]{2,1,0:T(1,128)S(1)} %all_to_all.15.slots_ref, f32[64,1,640]{2,1,0:T(1,128)S(1)} %all_to_all.17.inbox_ref), custom_call_target="tpu_custom_call" | custom-call | tf_op jit(solution)/shard_map/collect/pallas_call | solution.py:253
  (1 shorter events, 0.0 us)
Async XLA Ops:
  23.2 40.6 %slice-start = ((s8[12582912]{0:T(1024)(128)(4,1)}), s8[4194304]{0:T(1024)(128)(4,1)S(1)}, s32[]{:S(2)}) async-start(s8[12582912]{0:T(1024)(128)(4,1)} %bitcast.5), calls=%async_computation.3 | async-start | bytes 8388608
  23.2 40.6 %slice-start.1 = ((s8[12582912]{0:T(1024)(128)(4,1)}), s8[4194304]{0:T(1024)(128)(4,1)S(1)}, s32[]{:S(2)}) async-start(s8[12582912]{0:T(1024)(128)(4,1)} %bitcast.5), calls=%async_computation.4 | async-start | bytes 8388608
  23.2 40.6 %slice-start.2 = ((s8[12582912]{0:T(1024)(128)(4,1)}), s8[4194304]{0:T(1024)(128)(4,1)S(1)}, s32[]{:S(2)}) async-start(s8[12582912]{0:T(1024)(128)(4,1)} %bitcast.5), calls=%async_computation.5 | async-start | bytes 8388608
  24.4 39.5 %copy-start = (bf16[32,256,256]{2,1,0:T(8,128)(2,1)S(1)}, bf16[32,256,256]{2,1,0:T(8,128)(2,1)}, u32[]{:S(2)}) copy-start(bf16[32,256,256]{2,1,0:T(8,128)(2,1)} %diag_ref.3) | copy-start | bytes 12582916
  68.3 1.3 %collective-permute-start = (f32[2,32,256]{2,1,0:T(8,128)S(1)}, f32[2,32,256]{2,1,0:T(8,128)S(1)}, u32[]{:S(2)}, u32[]{:S(2)}) collective-permute-start(f32[2,32,256]{2,1,0:T(8,128)S(1)} %score.1.mine_ref), channel_id=1, source_target_pairs={{0,1},{1,0},{2,3},{3,2},{4,5},{5,4},{6,7},{7,6},{8,9},{9,8},{10,11... | collective-permute-start | bytes 196616 | tf_op jit(solution)/shard_map/ppermute | solution.py:242

commit v6 on v5

--- a/solution.py
+++ b/solution.py
@@ -198,7 +198,7 @@
     outbox, spot, noise_row, staged = pl.pallas_call(
         functools.partial(plan_kernel, owners, capacity),
         out_shape=(
-            jax.ShapeDtypeStruct((owners, 1, 128), jnp.int32),
+            jax.ShapeDtypeStruct((owners, 1, 8), jnp.int32),
             jax.ShapeDtypeStruct((want_kinds, row_count), jnp.int32),
             jax.ShapeDtypeStruct((1, width), jnp.float32),
             pltpu.VMEM(latent.shape, latent.dtype),

time: 87.7 us -> 87.7 us (level)
  no operation moved by 1% of the time
where the time goes in v6:
time: 87.7 us; the launch traced here: 87.4 us
  blocking collectives  74.9 us (85%)
  Pallas kernels  10.5 us (12%)
  waiting for transfers between devices  1.24 us (1%)
    all_to_all x3, blocking collectives, swap(): lax.all_to_all(values, 'blk', split_axis=0, concat_axis=0, tiled=True)  74.9 us
    pallas_call x1, Pallas kernels, body(): pl.pallas_call(functools.partial(score_kernel, 32), out_shape=jax.ShapeDt...  4.41 us
    pallas_call x1, Pallas kernels, body(): pl.pallas_call(functools.partial(term_kernel, draws, 32), out_shape=jax.S...  2.08 us
  transfers between devices with their start and end apart: 1, of which 1 were waited for; matrix products, arithmetic and copies ran while one was open for 0% of the time, Pallas kernels for 0%

profile of v6, /device:TPU:0, one launch (start us, length us, event | category | flops | bytes accessed | tf_op | source)
XLA Modules:
  0.0 87.4 jit_solution(11237037035760960047)
XLA Ops:
  0.7 1.7 %plan.1 = (s32[64,1,8]{2,1,0:T(1,128)S(1)}, s32[4,32]{1,0:T(4,128)S(1)}, f32[1,256]{1,0:T(1,128)S(1)}, bf16[256,16,256]{2,1,0:T(8,128)(2,1)S(1)}) custom-call(f32[1]{0:T(128)} %bitcast.4.noise_ref, s32[1,32]{1,0:T(1,128)} %bitcast.9, s32[3,32]{1,0:T(4,128)} %bitcast.8, s32[128,128]{1,0:T(8,128)} %bitcast.7, bf16[256,16,256]{2,1,0:T(8,128)(2,1)} %latent_hbm.1), custom_call_target="tpu_custom_call" | custom-call | tf_op jit(solution)/shard_map/plan/pallas_call | solution.py:198
  2.4 20.8 %all_to_all.15.slots_ref = s32[64,1,8]{2,1,0:T(1,128)S(1)} all-to-all(s32[64,1,8]{2,1,0:T(1,128)S(1)} %get-tuple-element.9), channel_id=1, replica_groups=mesh['blk'=64,'mc'=2] {'blk'}, dimensions={0} | all-to-all | bytes 4096 | tf_op jit(solution)/shard_map/all_to_all | solution.py:196
  23.2 0.0 slice-start
  23.2 0.0 slice-start.1
  23.2 0.0 slice-start.2
  23.2 1.2 %pack.1 = bf16[64,5,16,256]{3,2,1,0:T(8,128)(2,1)S(1)} custom-call(s32[64,1,8]{2,1,0:T(1,128)S(1)} %all_to_all.15.slots_ref, bf16[256,16,256]{2,1,0:T(8,128)(2,1)S(1)} %get-tuple-element.12.latent_ref), custom_call_target="tpu_custom_call" | custom-call | flops 99999997952 | bytes 100000000 | tf_op jit(solution)/shard_map/pack/pallas_call | solution.py:218
  24.4 0.0 copy-start
  24.4 39.4 %all_to_all.16.fetched_ref = bf16[64,5,16,256]{3,2,1,0:T(8,128)(2,1)S(1)} all-to-all(bf16[64,5,16,256]{3,2,1,0:T(8,128)(2,1)S(1)} %pack.1), channel_id=1, replica_groups=mesh['blk'=64,'mc'=2] {'blk'}, dimensions={0} | all-to-all | bytes 5242880 | tf_op jit(solution)/shard_map/all_to_all | solution.py:196
  63.9 0.0 slice-done
  63.9 0.0 slice-done.1
  63.9 0.0 slice-done.2
  63.9 0.0 copy-done
  63.9 4.4 %score.1.mine_ref = f32[2,32,256]{2,1,0:T(8,128)S(1)} custom-call(s32[4,32]{1,0:T(4,128)S(1)} %get-tuple-element.10.spot_ref, f32[1,256]{1,0:T(1,128)S(1)} %get-tuple-element.11.noise_ref, f32[32,256]{1,0:T(8,128)} %obs_ref.1, bf16[64,5,16,256]{3,2,1,0:T(8,128)(2,1)S(1)} %all_to_all.16.fetched_ref, bf16[32,256,256]{2,1,0:T(8,128)(2,1)S(1)} %copy-done, ...), custom_call_target="tpu_custom_call" | custom-call | tf_op jit(solution)/shard_map/score/pallas_call | solution.py:234
  68.3 0.1 collective-permute-start
  68.4 1.2 %collective-permute-done.other_ref = f32[2,32,256]{2,1,0:T(8,128)S(1)} collective-permute-done((f32[2,32,256]{2,1,0:T(8,128)S(1)}, f32[2,32,256]{2,1,0:T(8,128)S(1)}, u32[]{:S(2)}, u32[]{:S(2)}) %collective-permute-start) | collective-permute-done | bytes 65568 | tf_op jit(solution)/shard_map/ppermute | solution.py:242
  69.6 2.1 %terms.1 = f32[64,1,640]{2,1,0:T(1,128)S(1)} custom-call(s32[4,32]{1,0:T(4,128)S(1)} %get-tuple-element.10.spot_ref, f32[2,32,256]{2,1,0:T(8,128)S(1)} %score.1.mine_ref, f32[2,32,256]{2,1,0:T(8,128)S(1)} %collective-permute-done.other_ref, bf16[32,256,256]{2,1,0:T(8,128)(2,1)S(1)} %copy-done, bf16[32,3,256,256]{3,2,1,0:T(8,128)(2,1)S(1)} %bitcast.6), custom_call_target="tpu_custom_call" | custom-call | tf_op jit(solution)/shard_map/terms/pallas_call | solution.py:243
  71.7 14.6 %all_to_all.17.inbox_ref = f32[64,1,640]{2,1,0:T(1,128)S(1)} all-to-all(f32[64,1,640]{2,1,0:T(1,128)S(1)} %terms.1), channel_id=1, replica_groups=mesh['blk'=64,'mc'=2] {'blk'}, dimensions={0} | all-to-all | bytes 327680 | tf_op jit(solution)/shard_map/all_to_all | solution.py:196
  86.4 1.1 %collect.1 = f32[256,128]{1,0:T(8,128)} custom-call(s32[64,1,8]{2,1,0:T(1,128)S(1)} %all_to_all.15.slots_ref, f32[64,1,640]{2,1,0:T(1,128)S(1)} %all_to_all.17.inbox_ref), custom_call_target="tpu_custom_call" | custom-call | tf_op jit(solution)/shard_map/collect/pallas_call | solution.py:253
  (1 shorter events, 0.0 us)
Async XLA Ops:
  23.2 40.6 %slice-start = ((s8[12582912]{0:T(1024)(128)(4,1)}), s8[4194304]{0:T(1024)(128)(4,1)S(1)}, s32[]{:S(2)}) async-start(s8[12582912]{0:T(1024)(128)(4,1)} %bitcast.5), calls=%async_computation.3 | async-start | bytes 8388608
  23.2 40.6 %slice-start.1 = ((s8[12582912]{0:T(1024)(128)(4,1)}), s8[4194304]{0:T(1024)(128)(4,1)S(1)}, s32[]{:S(2)}) async-start(s8[12582912]{0:T(1024)(128)(4,1)} %bitcast.5), calls=%async_computation.4 | async-start | bytes 8388608
  23.2 40.6 %slice-start.2 = ((s8[12582912]{0:T(1024)(128)(4,1)}), s8[4194304]{0:T(1024)(128)(4,1)S(1)}, s32[]{:S(2)}) async-start(s8[12582912]{0:T(1024)(128)(4,1)} %bitcast.5), calls=%async_computation.5 | async-start | bytes 8388608
  24.4 39.5 %copy-start = (bf16[32,256,256]{2,1,0:T(8,128)(2,1)S(1)}, bf16[32,256,256]{2,1,0:T(8,128)(2,1)}, u32[]{:S(2)}) copy-start(bf16[32,256,256]{2,1,0:T(8,128)(2,1)} %diag_ref.3) | copy-start | bytes 12582916
  68.3 1.3 %collective-permute-start = (f32[2,32,256]{2,1,0:T(8,128)S(1)}, f32[2,32,256]{2,1,0:T(8,128)S(1)}, u32[]{:S(2)}, u32[]{:S(2)}) collective-permute-start(f32[2,32,256]{2,1,0:T(8,128)S(1)} %score.1.mine_ref), channel_id=1, source_target_pairs={{0,1},{1,0},{2,3},{3,2},{4,5},{5,4},{6,7},{7,6},{8,9},{9,8},{10,11... | collective-permute-start | bytes 196616 | tf_op jit(solution)/shard_map/ppermute | solution.py:242

commit v7 on v6

--- a/solution.py
+++ b/solution.py
@@ -174,12 +174,13 @@
     places = iota(jnp.int32, (per_owner, owners * capacity), 0).astype(jnp.float32)
     hot = (places == slots).astype(jnp.bfloat16)
     rest = jnp.concatenate([inbox_ref[:, 0, pl.ds(k * half, half)] for k in range(capacity)], axis=0)
-    total = jnp.zeros((per_owner, half), jnp.float32)
+    pieces = []
     for _ in range(3):
         piece = rest.astype(jnp.bfloat16)
         rest = rest - piece.astype(jnp.float32)
-        total = total + jnp.dot(hot, piece, preferred_element_type=jnp.float32)
-    out_ref[...] = total
+        pieces.append(piece)
+    total = jnp.dot(hot, jnp.concatenate(pieces, axis=1), preferred_element_type=jnp.float32)
+    out_ref[...] = total[:, :half] + total[:, half : 2 * half] + total[:, 2 * half :]
 
 
 def body(batch_ids, cond_ids, home, latent, diag_factor, cond_factor, obs, noise_prec):

time: 87.7 us -> 87.7 us (level)
  no operation moved by 1% of the time
where the time goes in v7:
time: 87.7 us; the launch traced here: 87.4 us
  blocking collectives  74.9 us (85%)
  Pallas kernels  10.4 us (12%)
  waiting for transfers between devices  1.24 us (1%)
    all_to_all x3, blocking collectives, swap(): lax.all_to_all(values, 'blk', split_axis=0, concat_axis=0, tiled=True)  74.9 us
    pallas_call x1, Pallas kernels, body(): pl.pallas_call(functools.partial(score_kernel, 32), out_shape=jax.ShapeDt...  4.4 us
    pallas_call x1, Pallas kernels, body(): pl.pallas_call(functools.partial(term_kernel, draws, 32), out_shape=jax.S...  2.08 us
  transfers between devices with their start and end apart: 1, of which 1 were waited for; matrix products, arithmetic and copies ran while one was open for 0% of the time, Pallas kernels for 0%

profile of v7, /device:TPU:0, one launch (start us, length us, event | category | flops | bytes accessed | tf_op | source)
XLA Modules:
  0.0 87.4 jit_solution(4109474235907207367)
XLA Ops:
  0.7 1.7 %plan.1 = (s32[64,1,8]{2,1,0:T(1,128)S(1)}, s32[4,32]{1,0:T(4,128)S(1)}, f32[1,256]{1,0:T(1,128)S(1)}, bf16[256,16,256]{2,1,0:T(8,128)(2,1)S(1)}) custom-call(f32[1]{0:T(128)} %bitcast.4.noise_ref, s32[1,32]{1,0:T(1,128)} %bitcast.9, s32[3,32]{1,0:T(4,128)} %bitcast.8, s32[128,128]{1,0:T(8,128)} %bitcast.7, bf16[256,16,256]{2,1,0:T(8,128)(2,1)} %latent_hbm.1), custom_call_target="tpu_custom_call" | custom-call | tf_op jit(solution)/shard_map/plan/pallas_call | solution.py:199
  2.4 20.8 %all_to_all.15.slots_ref = s32[64,1,8]{2,1,0:T(1,128)S(1)} all-to-all(s32[64,1,8]{2,1,0:T(1,128)S(1)} %get-tuple-element.9), channel_id=1, replica_groups=mesh['blk'=64,'mc'=2] {'blk'}, dimensions={0} | all-to-all | bytes 4096 | tf_op jit(solution)/shard_map/all_to_all | solution.py:197
  23.2 0.0 slice-start
  23.2 0.0 slice-start.1
  23.2 0.0 slice-start.2
  23.2 1.2 %pack.1 = bf16[64,5,16,256]{3,2,1,0:T(8,128)(2,1)S(1)} custom-call(s32[64,1,8]{2,1,0:T(1,128)S(1)} %all_to_all.15.slots_ref, bf16[256,16,256]{2,1,0:T(8,128)(2,1)S(1)} %get-tuple-element.12.latent_ref), custom_call_target="tpu_custom_call" | custom-call | flops 99999997952 | bytes 100000000 | tf_op jit(solution)/shard_map/pack/pallas_call | solution.py:219
  24.4 0.0 copy-start
  24.4 39.4 %all_to_all.16.fetched_ref = bf16[64,5,16,256]{3,2,1,0:T(8,128)(2,1)S(1)} all-to-all(bf16[64,5,16,256]{3,2,1,0:T(8,128)(2,1)S(1)} %pack.1), channel_id=1, replica_groups=mesh['blk'=64,'mc'=2] {'blk'}, dimensions={0} | all-to-all | bytes 5242880 | tf_op jit(solution)/shard_map/all_to_all | solution.py:197
  63.9 0.0 slice-done
  63.9 0.0 slice-done.1
  63.9 0.0 slice-done.2
  63.9 0.0 copy-done
  63.9 4.4 %score.1.mine_ref = f32[2,32,256]{2,1,0:T(8,128)S(1)} custom-call(s32[4,32]{1,0:T(4,128)S(1)} %get-tuple-element.10.spot_ref, f32[1,256]{1,0:T(1,128)S(1)} %get-tuple-element.11.noise_ref, f32[32,256]{1,0:T(8,128)} %obs_ref.1, bf16[64,5,16,256]{3,2,1,0:T(8,128)(2,1)S(1)} %all_to_all.16.fetched_ref, bf16[32,256,256]{2,1,0:T(8,128)(2,1)S(1)} %copy-done, ...), custom_call_target="tpu_custom_call" | custom-call | tf_op jit(solution)/shard_map/score/pallas_call | solution.py:235
  68.3 0.1 collective-permute-start
  68.4 1.2 %collective-permute-done.other_ref = f32[2,32,256]{2,1,0:T(8,128)S(1)} collective-permute-done((f32[2,32,256]{2,1,0:T(8,128)S(1)}, f32[2,32,256]{2,1,0:T(8,128)S(1)}, u32[]{:S(2)}, u32[]{:S(2)}) %collective-permute-start) | collective-permute-done | bytes 65568 | tf_op jit(solution)/shard_map/ppermute | solution.py:243
  69.6 2.1 %terms.1 = f32[64,1,640]{2,1,0:T(1,128)S(1)} custom-call(s32[4,32]{1,0:T(4,128)S(1)} %get-tuple-element.10.spot_ref, f32[2,32,256]{2,1,0:T(8,128)S(1)} %score.1.mine_ref, f32[2,32,256]{2,1,0:T(8,128)S(1)} %collective-permute-done.other_ref, bf16[32,256,256]{2,1,0:T(8,128)(2,1)S(1)} %copy-done, bf16[32,3,256,256]{3,2,1,0:T(8,128)(2,1)S(1)} %bitcast.6), custom_call_target="tpu_custom_call" | custom-call | tf_op jit(solution)/shard_map/terms/pallas_call | solution.py:244
  71.7 14.7 %all_to_all.17.inbox_ref = f32[64,1,640]{2,1,0:T(1,128)S(1)} all-to-all(f32[64,1,640]{2,1,0:T(1,128)S(1)} %terms.1), channel_id=1, replica_groups=mesh['blk'=64,'mc'=2] {'blk'}, dimensions={0} | all-to-all | bytes 327680 | tf_op jit(solution)/shard_map/all_to_all | solution.py:197
  86.4 1.0 %collect.1 = f32[256,128]{1,0:T(8,128)} custom-call(s32[64,1,8]{2,1,0:T(1,128)S(1)} %all_to_all.15.slots_ref, f32[64,1,640]{2,1,0:T(1,128)S(1)} %all_to_all.17.inbox_ref), custom_call_target="tpu_custom_call" | custom-call | tf_op jit(solution)/shard_map/collect/pallas_call | solution.py:254
  (1 shorter events, 0.0 us)
Async XLA Ops:
  23.2 40.6 %slice-start = ((s8[12582912]{0:T(1024)(128)(4,1)}), s8[4194304]{0:T(1024)(128)(4,1)S(1)}, s32[]{:S(2)}) async-start(s8[12582912]{0:T(1024)(128)(4,1)} %bitcast.5), calls=%async_computation.3 | async-start | bytes 8388608
  23.2 40.6 %slice-start.1 = ((s8[12582912]{0:T(1024)(128)(4,1)}), s8[4194304]{0:T(1024)(128)(4,1)S(1)}, s32[]{:S(2)}) async-start(s8[12582912]{0:T(1024)(128)(4,1)} %bitcast.5), calls=%async_computation.4 | async-start | bytes 8388608
  23.2 40.6 %slice-start.2 = ((s8[12582912]{0:T(1024)(128)(4,1)}), s8[4194304]{0:T(1024)(128)(4,1)S(1)}, s32[]{:S(2)}) async-start(s8[12582912]{0:T(1024)(128)(4,1)} %bitcast.5), calls=%async_computation.5 | async-start | bytes 8388608
  24.4 39.5 %copy-start = (bf16[32,256,256]{2,1,0:T(8,128)(2,1)S(1)}, bf16[32,256,256]{2,1,0:T(8,128)(2,1)}, u32[]{:S(2)}) copy-start(bf16[32,256,256]{2,1,0:T(8,128)(2,1)} %diag_ref.3) | copy-start | bytes 12582916
  68.3 1.3 %collective-permute-start = (f32[2,32,256]{2,1,0:T(8,128)S(1)}, f32[2,32,256]{2,1,0:T(8,128)S(1)}, u32[]{:S(2)}, u32[]{:S(2)}) collective-permute-start(f32[2,32,256]{2,1,0:T(8,128)S(1)} %score.1.mine_ref), channel_id=1, source_target_pairs={{0,1},{1,0},{2,3},{3,2},{4,5},{5,4},{6,7},{7,6},{8,9},{9,8},{10,11... | collective-permute-start | bytes 196616 | tf_op jit(solution)/shard_map/ppermute | solution.py:243
